TPU v7x, 256 devices: a whole 4x4x8 slice. The times are simulated.
256 devices in a mesh: lat: 8 (over z), lon: 32 (over x, y, core).
Axes of the slice: x: 4, y: 4, z: 8, core: 2. Of those that a mesh axis runs over, the one named last changes fastest.
Arguments:
- state: float32 [80, 3, 64, 4096], P(None, None, 'lat', 'lon'), may hold values from -6 to 6
- east_courant: float32 [64, 4096], P('lat', 'lon'), may hold values from -0.4 to 0.4
- north_courant: float32 [64, 4096], P('lat', 'lon'), may hold values from -0.4 to 0.4
- obs_cell: int32 [4, 256], replicated, may hold values from 0 to 262143, as said below
- obs_value: float32 [4, 256], replicated, may hold values from -6 to 6
- obs_error_var: float32 [4, 256], replicated, may hold values from 0.25 to 4
- loc_lat: float32 [9], replicated, may hold values from 0.25 to 1
- loc_lon: float32 [129], replicated, may hold values from 0.25 to 1
Outputs:
- analysis: float32 [80, 3, 64, 4096], P(None, None, 'lat', 'lon')
Inputs may be any that keep to these rules, and one draw needn't show every extreme that they name: obs_cell holds row * 4096 + column of a cell of the 64 x 4096 grid.
All inputs are finite; a program needn't handle non-finite values.
Results may differ from a plain program's by a relative error of at most 0.0001.
Values sent between devices are 32-bit elements; how exact they have to be, the bound alone decides.
A program may use at most 64 MiB of HBM per device.

v0:
```python
import jax
import jax.numpy as jnp
from jax import lax
from jax.sharding import PartitionSpec as P

diffusion_number = 0.2
variance_eps = 1e-06


def passed_along(value, axis, by):
    count = lax.axis_size(axis)
    pairs = [(i, i + by) for i in range(count) if 0 <= i + by < count]
    return lax.ppermute(value, axis, pairs)


def from_behind(block, axis, distance):
    devices = range(lax.axis_size(axis))
    route = [((i - distance) % len(devices), i) for i in devices]
    return lax.ppermute(block, axis, route)


def padded(cells, sides, width, closed):
    for axis, dim in sides:
        count = lax.axis_size(axis)
        ends = count if closed else count - 1
        head = lax.slice_in_dim(cells, 0, width, axis=dim)
        tail = lax.slice_in_dim(cells, cells.shape[dim] - width, cells.shape[dim], axis=dim)
        cells = jnp.concatenate(
            [
                lax.ppermute(tail, axis, [(i, (i + 1) % count) for i in range(ends)]),
                cells,
                lax.ppermute(head, axis, [((i + 1) % count, i) for i in range(ends)]),
            ],
            axis=dim,
        )
    return cells


def obs_increments(priors, values, error_var, members):
    prior_mean = jnp.mean(priors, axis=0)
    anomaly = priors - prior_mean
    variance = jnp.sum(anomaly * anomaly, axis=0) / (members - 1) + variance_eps
    post_var = 1.0 / (1.0 / variance + 1.0 / error_var)
    post_mean = post_var * (prior_mean / variance + values / error_var)
    return (anomaly, variance, post_mean + jnp.sqrt(post_var / variance) * anomaly - priors)


def collect(local_priors):
    column = (
        local_priors + passed_along(local_priors, "lat", 1) + passed_along(local_priors, "lat", -1)
    )
    return column + from_behind(column, "lon", 1) + from_behind(column, "lon", -1)


def on_device(
    state, east_courant, north_courant, obs_cell, obs_value, obs_error_var, loc_lat, loc_lon
):
    members, channels, tile_rows, tile_cols = state.shape
    cell_count = tile_rows * tile_cols
    batches, obs_count = obs_cell.shape
    lat_padded = padded(state, (("lat", 2),), 1, False)
    lon_padded = padded(state, (("lon", 3),), 1, True)
    north_side = lat_padded[:, :, 2:, :]
    south_side = lat_padded[:, :, :-2, :]
    east_side = lon_padded[:, :, :, 2:]
    west_side = lon_padded[:, :, :, :-2]
    advected = (
        state
        - 0.5 * east_courant * (east_side - west_side)
        - 0.5 * north_courant * (north_side - south_side)
        + diffusion_number * (east_side + west_side + north_side + south_side - 4.0 * state)
    )
    fields = [advected[:, index].reshape(members, cell_count) for index in range(channels)]
    first_row = lax.axis_index("lat") * tile_rows
    first_col = lax.axis_index("lon") * tile_cols
    grid_cols = tile_cols * lax.axis_size("lon")
    lat_table = jnp.concatenate([loc_lat, jnp.zeros((1,), jnp.float32)])
    lon_table = jnp.concatenate([loc_lon, jnp.zeros((1,), jnp.float32)])
    row_ids = first_row + jnp.arange(tile_rows, dtype=jnp.int32)
    col_ids = first_col + jnp.arange(tile_cols, dtype=jnp.int32)
    highest = lax.Precision.HIGHEST

    def owned_spots(cells):
        row_offset = cells // grid_cols - first_row
        col_offset = cells % grid_cols - first_col
        owned = (
            (row_offset >= 0)
            & (row_offset < tile_rows)
            & (col_offset >= 0)
            & (col_offset < tile_cols)
        )
        spots = jnp.where(owned, row_offset * tile_cols + col_offset, 0)
        return (spots, owned)

    def gain_for(field, anomaly, variance, weights):
        field_anom = field - jnp.mean(field, axis=0)
        covar = lax.dot_general(
            anomaly, field_anom, (((0,), (0,)), ((), ())), precision=highest
        ) / (members - 1)
        return covar * weights / variance[:, None]

    def plain_step(fields, increments, anomaly, variance, weights, batch_index):
        updated = [
            field
            + jnp.dot(increments, gain_for(field, anomaly, variance, weights), precision=highest)
            for field in fields
        ]
        if batch_index + 1 < batches:
            spots, owned = owned_spots(obs_cell[batch_index + 1])
            local_priors = jnp.where(owned[None, :], jnp.take(updated[0], spots, axis=1), 0.0)
            return (updated, collect(local_priors))
        return (updated, None)

    spots, owned = owned_spots(obs_cell[0])
    priors = collect(jnp.where(owned[None, :], jnp.take(fields[0], spots, axis=1), 0.0))
    for batch_index in range(batches):
        locality_cells = obs_cell[batch_index]
        lat_obs = locality_cells // grid_cols
        lon_obs = locality_cells % grid_cols
        lat_dist = jnp.minimum(jnp.abs(row_ids[None, :] - lat_obs[:, None]), tile_rows + 1)
        lon_gap = (col_ids[None, :] - lon_obs[:, None]) % grid_cols
        lon_dist = jnp.minimum(jnp.minimum(lon_gap, grid_cols - lon_gap), tile_cols + 1)
        lat_weight = jnp.take(lat_table, lat_dist)
        lon_weight = jnp.take(lon_table, lon_dist)
        weights = (lat_weight[:, :, None] * lon_weight[:, None, :]).reshape(obs_count, cell_count)
        anomaly, variance, increments = obs_increments(
            priors, obs_value[batch_index], obs_error_var[batch_index], members
        )
        fields, priors = plain_step(fields, increments, anomaly, variance, weights, batch_index)
    return jnp.stack([field.reshape(members, tile_rows, tile_cols) for field in fields], axis=1)


def solution(mesh):
    in_specs = (
        P(None, None, "lat", "lon"),
        P("lat", "lon"),
        P("lat", "lon"),
        P(),
        P(),
        P(),
        P(),
        P(),
    )
    out_specs = P(None, None, "lat", "lon")
    return jax.shard_map(
        on_device, mesh=mesh, in_specs=in_specs, out_specs=out_specs, check_vma=False
    )
```

profile of v0, /device:TPU:1, one launch (start us, length us, event | category | flops | bytes accessed | tf_op | source)
XLA Modules:
  0.0 948.2 jit_solution(14226417499167341401)
XLA Ops:
  0.0 1.8 fusion.175
  2.8 3.2 collective-permute-start
  7.0 1.7 fusion.176
  9.4 1.3 collective-permute-start.2
  11.3 4.6 collective-permute-start.3
  20.8 202.2 %gather_fusion.3 = f32[32768]{0:T(1024)S(1)} fusion(f32[130]{0:T(256)S(1)} %pad_maximum_fusion.5, s32[32768]{0:T(1024)S(1)} %get-tuple-element.67), kind=kCustom, calls=%fused_computation.5.clone | custom fusion | bytes 393216 | tf_op jit(solution)/shard_map/jit(_take)/gather | solution.py:124
  223.1 202.2 %gather_fusion.5 = f32[32768]{0:T(1024)S(1)} fusion(f32[130]{0:T(256)S(1)} %pad_maximum_fusion.5, s32[32768]{0:T(1024)S(1)} %get-tuple-element.68), kind=kCustom, calls=%fused_computation.6.clone | custom fusion | bytes 393216 | tf_op jit(solution)/shard_map/jit(_take)/gather | solution.py:124
  425.3 202.2 %gather_fusion.1 = f32[32768]{0:T(1024)S(1)} fusion(f32[130]{0:T(256)S(1)} %pad_maximum_fusion.5, s32[32768]{0:T(1024)S(1)} %get-tuple-element.69), kind=kCustom, calls=%fused_computation.1.clone | custom fusion | bytes 393216 | tf_op jit(solution)/shard_map/jit(_take)/gather | solution.py:124
  627.6 202.2 %gather_fusion.7 = f32[32768]{0:T(1024)S(1)} fusion(f32[130]{0:T(256)S(1)} %pad_maximum_fusion.5, s32[32768]{0:T(1024)S(1)} %get-tuple-element.66), kind=kCustom, calls=%fused_computation.7.clone | custom fusion | bytes 393216 | tf_op jit(solution)/shard_map/jit(_take)/gather | solution.py:124
  833.1 6.3 select_select_fusion
  839.4 1.3 broadcast_multiply_fusion.3
  840.7 1.3 broadcast_multiply_fusion.2
  842.1 1.3 broadcast_multiply_fusion.1
  843.4 1.3 broadcast_multiply_fusion
  853.1 2.5 collective-permute-start.4
  855.6 1.3 collective-permute-start.5
  857.5 4.0 collective-permute-done.5
  861.6 3.4 collective-permute-start.6
  865.0 2.4 collective-permute-start.7
  867.7 2.2 collective-permute-done.7
  870.9 1.2 fusion.12
  874.8 4.8 collective-permute-start.8
  879.5 1.3 collective-permute-start.9
  880.8 1.2 fusion.16
  885.4 2.4 collective-permute-start.10
  887.8 4.1 collective-permute-start.11
  897.1 4.8 collective-permute-start.12
  901.9 1.5 collective-permute-start.13
  908.9 7.0 collective-permute-start.15
  921.2 3.6 collective-permute-start.16
  924.8 1.3 collective-permute-start.17
  931.0 8.1 collective-permute-start.19
  (201 shorter events, 56.8 us)
Async XLA Ops:
  2.8 843.2 %collective-permute-start = (f32[80,3,8,1]{0,2,3,1:T(8,128)}, f32[80,3,8,1]{0,2,3,1:T(8,128)}, u32[]{:S(2)}, u32[]{:S(2)}) collective-permute-start(f32[80,3,8,1]{0,2,3,1:T(8,128)} %copy.38), channel_id=1, source_target_pairs={{1,0},{2,1},{3,2},{4,3},{5,4},{6,5},{7,6},{8,7},{9,8},{10,9},{11,1... | collective-permute-start | bytes 23048 | tf_op jit(solution)/shard_map/ppermute | solution.py:32
  7.0 840.2 %collective-permute-start.1 = (f32[80,3,8,1]{0,2,3,1:T(8,128)}, f32[80,3,8,1]{0,2,3,1:T(8,128)}, u32[]{:S(2)}, u32[]{:S(2)}) collective-permute-start(f32[80,3,8,1]{0,2,3,1:T(8,128)} %copy.39), channel_id=1, source_target_pairs={{0,1},{1,2},{2,3},{3,4},{4,5},{5,6},{6,7},{7,8},{8,9},{9,10},{10,1... | collective-permute-start | bytes 23048 | tf_op jit(solution)/shard_map/ppermute | solution.py:30
  9.4 839.0 %collective-permute-start.2 = (f32[80,3,1,128]{3,0,2,1:T(8,128)}, f32[80,3,1,128]{3,0,2,1:T(8,128)}, u32[]{:S(2)}, u32[]{:S(2)}) collective-permute-start(f32[80,3,1,128]{3,0,2,1:T(8,128)} %copy.40), channel_id=1, source_target_pairs={{32,0},{64,32},{96,64},{128,96},{160,128},{192,160},{224,192},{33,... | collective-permute-start | bytes 368648 | tf_op jit(solution)/shard_map/ppermute | solution.py:32
  11.3 838.1 %collective-permute-start.3 = (f32[80,3,1,128]{3,0,2,1:T(8,128)}, f32[80,3,1,128]{3,0,2,1:T(8,128)}, u32[]{:S(2)}, u32[]{:S(2)}) collective-permute-start(f32[80,3,1,128]{3,0,2,1:T(8,128)} %copy.41), channel_id=1, source_target_pairs={{0,32},{32,64},{64,96},{96,128},{128,160},{160,192},{192,224},{1,3... | collective-permute-start | bytes 368648 | tf_op jit(solution)/shard_map/ppermute | solution.py:30
  16.7 3.2 copy-start.34
  627.6 202.3 %copy-start.5 = (f32[9]{0:T(128)S(1)}, f32[9]{0:T(128)}, u32[]{:S(2)}) copy-start(f32[9]{0:T(128)} %param.20) | copy-start | bytes 112
  627.6 204.9 %copy-start.24 = (s32[256]{0:T(256)S(1)}, s32[256]{0:T(256)}, u32[]{:S(2)}) copy-start(s32[256]{0:T(256)} %get-tuple-element.106) | copy-start | bytes 3076
  627.6 204.9 %copy-start.25 = (s32[256]{0:T(256)S(1)}, s32[256]{0:T(256)}, u32[]{:S(2)}) copy-start(s32[256]{0:T(256)} %get-tuple-element.21) | copy-start | bytes 3076
  627.6 204.9 %copy-start.26 = (s32[256]{0:T(256)S(1)}, s32[256]{0:T(256)}, u32[]{:S(2)}) copy-start(s32[256]{0:T(256)} %get-tuple-element.102) | copy-start | bytes 3076
  847.1 3.3 copy-start
  851.5 1.4 copy-start.18
  851.5 1.4 copy-start.22
  851.9 19.0 %copy-start.4 = (f32[256,8,128]{2,1,0:T(8,128)S(1)}, f32[256,8,128]{2,1,0:T(8,128)}, u32[]{:S(2)}) copy-start(f32[256,8,128]{2,1,0:T(8,128)} %broadcast_multiply_fusion.3) | copy-start | bytes 3145732
  853.1 4.5 collective-permute-start.4
  855.6 5.9 collective-permute-start.5
  861.6 6.0 collective-permute-start.6
  865.0 4.8 collective-permute-start.7
  874.8 10.4 %collective-permute-start.8 = (f32[80,256]{0,1:T(8,128)S(1)}, f32[80,256]{0,1:T(8,128)S(1)}, u32[]{:S(2)}, u32[]{:S(2)}) collective-permute-start(f32[80,256]{0,1:T(8,128)S(1)} %bitcast_select_fusion.5), channel_id=1, source_target_pairs={{0,32},{32,64},{64,96},{96,128},{128,160},{160,192},{192,224},{1,3... | collective-permute-start | bytes 245768 | tf_op jit(solution)/shard_map/ppermute | solution.py:13
  879.5 5.7 collective-permute-start.9
  885.1 8.1 copy-start.3
  885.4 7.3 collective-permute-start.10
  887.8 5.1 collective-permute-start.11
  897.1 10.5 %collective-permute-start.12 = (f32[80,256]{0,1:T(8,128)S(1)}, f32[80,256]{0,1:T(8,128)S(1)}, u32[]{:S(2)}, u32[]{:S(2)}) collective-permute-start(f32[80,256]{0,1:T(8,128)S(1)} %bitcast_select_fusion.3), channel_id=1, source_target_pairs={{0,32},{32,64},{64,96},{96,128},{128,160},{160,192},{192,224},{1,3... | collective-permute-start | bytes 245768 | tf_op jit(solution)/shard_map/ppermute | solution.py:13
  901.9 6.0 collective-permute-start.13
  907.6 9.7 %copy-start.2 = (f32[256,8,128]{2,1,0:T(8,128)S(1)}, f32[256,8,128]{2,1,0:T(8,128)}, u32[]{:S(2)}) copy-start(f32[256,8,128]{2,1,0:T(8,128)} %broadcast_multiply_fusion.1) | copy-start | bytes 3145732
  908.0 8.7 collective-permute-start.14
  908.9 8.0 collective-permute-start.15
  921.2 9.2 collective-permute-start.16
  924.8 5.7 collective-permute-start.17
  930.4 10.1 %copy-start.1 = (f32[256,8,128]{2,1,0:T(8,128)S(1)}, f32[256,8,128]{2,1,0:T(8,128)}, u32[]{:S(2)}) copy-start(f32[256,8,128]{2,1,0:T(8,128)} %broadcast_multiply_fusion) | copy-start | bytes 3145732
  930.7 9.2 collective-permute-start.18
  931.0 9.1 collective-permute-start.19
  (26 other events, 19.3 us)
where the time goes:
time: 964 us; the launch traced here: 948 us
  local copies, waits for them, and re-layouts  832 us (86%)
  starting transfers between devices  58.8 us (6%)
  matrix products  25.2 us (3%)
  other arithmetic  20.2 us (2%)
  waiting for transfers between devices  10.5 us (1%)
    gather x4, local copies, waits for them, and re-layouts, on_device(): lon_weight = jnp.take(lon_table, lon_dist)  809 us
    ppermute x8, starting transfers between devices, from_behind(): return lax.ppermute(block, axis, route)  28.6 us
    ppermute x8, starting transfers between devices, passed_along(): return lax.ppermute(value, axis, pairs)  21 us
  transfers between devices with their start and end apart: 20, of which 13 were waited for; matrix products, arithmetic and copies ran while one was open for 89% of the time, Pallas kernels for 0%

commit v1 on v0

v1 whole, which is shorter than its diff:
```python
import jax
import jax.numpy as jnp
from jax import lax
from jax.sharding import PartitionSpec as P

diffusion_number = 0.2
variance_eps = 1e-06
highest = lax.Precision.HIGHEST


def shifted(value, axis, by, closed):
    count = lax.axis_size(axis)
    pairs = [(i, (i + by) % count) for i in range(count) if closed or 0 <= i + by < count]
    return lax.ppermute(value, axis, pairs)


def padded(cells, axis, dim, closed):
    last = cells.shape[dim] - 1
    head = lax.slice_in_dim(cells, 0, 1, axis=dim)
    tail = lax.slice_in_dim(cells, last, last + 1, axis=dim)
    return jnp.concatenate(
        [shifted(tail, axis, 1, closed), cells, shifted(head, axis, -1, closed)], axis=dim
    )


def obs_increments(priors, values, error_var, members):
    prior_mean = jnp.mean(priors, axis=0)
    anomaly = priors - prior_mean
    variance = jnp.sum(anomaly * anomaly, axis=0) / (members - 1) + variance_eps
    post_var = 1.0 / (1.0 / variance + 1.0 / error_var)
    post_mean = post_var * (prior_mean / variance + values / error_var)
    return (anomaly, variance, post_mean + jnp.sqrt(post_var / variance) * anomaly - priors)


def collect(local_priors):
    column = (
        local_priors
        + shifted(local_priors, "lat", 1, False)
        + shifted(local_priors, "lat", -1, False)
    )
    return column + shifted(column, "lon", 1, True) + shifted(column, "lon", -1, True)


def looked_up(table, distance):
    steps = jnp.arange(table.shape[0], dtype=jnp.int32)[:, None, None]
    return jnp.sum(jnp.where(distance[None] == steps, table[:, None, None], 0.0), axis=0)


def general(
    state, east_courant, north_courant, obs_cell, obs_value, obs_error_var, loc_lat, loc_lon
):
    members, channels, tile_rows, tile_cols = state.shape
    cell_count = tile_rows * tile_cols
    batches, obs_count = obs_cell.shape
    lat_padded = padded(state, "lat", 2, False)
    lon_padded = padded(state, "lon", 3, True)
    north_side = lat_padded[:, :, 2:, :]
    south_side = lat_padded[:, :, :-2, :]
    east_side = lon_padded[:, :, :, 2:]
    west_side = lon_padded[:, :, :, :-2]
    advected = (
        state
        - 0.5 * east_courant * (east_side - west_side)
        - 0.5 * north_courant * (north_side - south_side)
        + diffusion_number * (east_side + west_side + north_side + south_side - 4.0 * state)
    )
    first_row = lax.axis_index("lat") * tile_rows
    first_col = lax.axis_index("lon") * tile_cols
    grid_cols = tile_cols * lax.axis_size("lon")
    row_ids = first_row + jnp.arange(tile_rows, dtype=jnp.int32)
    col_ids = first_col + jnp.arange(tile_cols, dtype=jnp.int32)

    def step(batch, field):
        cells = lax.dynamic_index_in_dim(obs_cell, batch, 0, False)
        values = lax.dynamic_index_in_dim(obs_value, batch, 0, False)
        error_var = lax.dynamic_index_in_dim(obs_error_var, batch, 0, False)
        obs_row, obs_col = cells // grid_cols, cells % grid_cols
        spot = (obs_row - first_row) * tile_cols + obs_col - first_col
        owned = (obs_col >= first_col) & (obs_col < first_col + tile_cols)
        spot = jnp.where(owned, spot, -1)
        chosen = (jnp.arange(cell_count, dtype=jnp.int32)[:, None] == spot[None, :]).astype(
            jnp.float32
        )
        priors = collect(jnp.dot(field[:, :cell_count], chosen, precision=highest))
        lat_dist = jnp.abs(row_ids[None, :] - obs_row[:, None])
        gap = (col_ids[None, :] - obs_col[:, None]) % grid_cols
        lon_dist = jnp.minimum(gap, grid_cols - gap)
        weights = (
            looked_up(loc_lat, lat_dist)[:, :, None] * looked_up(loc_lon, lon_dist)[:, None, :]
        ).reshape(obs_count, cell_count)
        anomaly, variance, increments = obs_increments(priors, values, error_var, members)
        field_anom = field - jnp.mean(field, axis=0)
        covar = lax.dot_general(
            anomaly, field_anom, (((0,), (0,)), ((), ())), precision=highest
        ) / (members - 1)
        gain = covar * jnp.tile(weights, (1, channels)) / variance[:, None]
        return field + jnp.dot(increments, gain, precision=highest)

    field = lax.fori_loop(0, batches, step, advected.reshape(members, channels * cell_count))
    return field.reshape(state.shape)


def solution(mesh):
    in_specs = (
        P(None, None, "lat", "lon"),
        P("lat", "lon"),
        P("lat", "lon"),
        P(),
        P(),
        P(),
        P(),
        P(),
    )
    out_specs = P(None, None, "lat", "lon")
    return jax.shard_map(
        general, mesh=mesh, in_specs=in_specs, out_specs=out_specs, check_vma=False
    )
```

time: 964 us -> 139 us (0.14)
  the two profiles are of different devices: /device:TPU:1 before, /device:TPU:96 now
where the time goes in v1:
time: 139 us; the launch traced here: 138 us
  starting transfers between devices  43.9 us (32%)
  matrix products  31.5 us (23%)
  local copies, waits for them, and re-layouts  22.8 us (16%)
  other arithmetic  20.2 us (15%)
  waiting for transfers between devices  19 us (14%)
    ppermute x20, starting transfers between devices, shifted(): return lax.ppermute(value, axis, pairs)  43.9 us
    dot_general x4, matrix products, step(): lax.dot_general(anomaly, field_anom, (((0,), (0,)), ((), ())), precision=...  20.5 us
    ppermute x20, waiting for transfers between devices, shifted(): return lax.ppermute(value, axis, pairs)  19 us
    another operation x8, local copies, waits for them, and re-layouts, step(): gain = covar * jnp.tile(weights, (1, channels)) / variance[:, None]  15.3 us
    dot_general x4, matrix products, step(): return field + jnp.dot(increments, gain, precision=highest)  8.99 us
    reduce_sum x8, other arithmetic, looked_up(): jnp.sum(jnp.where(distance[None] == steps, table[:, None, None], 0.0), ax...  7.38 us
    mul x4, other arithmetic, step(): looked_up(loc_lat, lat_dist)[:, :, None]  4.28 us
    slice x2, local copies, waits for them, and re-layouts, padded(): tail = lax.slice_in_dim(cells, last, last + 1, axis=dim)  3.99 us
  transfers between devices with their start and end apart: 20, of which 6 were waited for; matrix products, arithmetic and copies ran while one was open for 23% of the time, Pallas kernels for 0%

profile of v1, /device:TPU:96, one launch (start us, length us, event | category | flops | bytes accessed | tf_op | source)
XLA Modules:
  0.0 138.3 jit_solution(815768678009738841)
XLA Ops:
  0.0 1.9 %fusion.24 = (f32[80,3,1,128]{3,2,1,0:T(1,128)S(1)}, f32[80,3,1,128]{3,2,1,0:T(1,128)S(1)}) fusion(f32[80,3,8,128]{3,2,1,0:T(8,128)} %param.10), kind=kLoop, calls=%fused_computation.72 | loop fusion | bytes 491520 | tf_op jit(solution)/shard_map/slice | solution.py:20
  2.0 2.0 %collective-permute-start.6 = (f32[80,3,1,128]{3,0,2,1:T(8,128)S(1)}, f32[80,3,1,128]{3,0,2,1:T(8,128)S(1)}, u32[]{:S(2)}, u32[]{:S(2)}) collective-permute-start(f32[80,3,1,128]{3,0,2,1:T(8,128)S(1)} %copy.30), channel_id=1, source_target_pairs={{32,0},{64,32},{96,64},{128,96},{160,128},{192,160},{224,192},{33,... | collective-permute-start | bytes 368648 | tf_op jit(solution)/shard_map/ppermute | solution.py:14
  4.0 5.0 %collective-permute-start.7 = (f32[80,3,1,128]{3,0,2,1:T(8,128)S(1)}, f32[80,3,1,128]{3,0,2,1:T(8,128)S(1)}, u32[]{:S(2)}, u32[]{:S(2)}) collective-permute-start(f32[80,3,1,128]{3,0,2,1:T(8,128)S(1)} %copy.31), channel_id=1, source_target_pairs={{0,32},{32,64},{64,96},{96,128},{128,160},{160,192},{192,224},{1,3... | collective-permute-start | bytes 368648 | tf_op jit(solution)/shard_map/ppermute | solution.py:14
  9.1 2.1 %fusion.23 = (f32[80,3,8,1]{3,2,1,0:T(8,128)S(1)}, f32[80,3,8,1]{3,2,1,0:T(8,128)S(1)}) fusion(f32[80,3,8,128]{3,2,1,0:T(8,128)} %param.10), kind=kLoop, calls=%fused_computation.71 | loop fusion | bytes 30720 | tf_op jit(solution)/shard_map/slice | solution.py:20
  11.5 4.3 %collective-permute-start.4 = (f32[80,3,8,1]{0,2,3,1:T(8,128)S(1)}, f32[80,3,8,1]{0,2,3,1:T(8,128)S(1)}, u32[]{:S(2)}, u32[]{:S(2)}) collective-permute-start(f32[80,3,8,1]{0,2,3,1:T(8,128)S(1)} %copy.28), channel_id=1, source_target_pairs={{0,31},{1,0},{2,1},{3,2},{4,3},{5,4},{6,5},{7,6},{8,7},{9,8},{10,9... | collective-permute-start | bytes 23048 | tf_op jit(solution)/shard_map/ppermute | solution.py:14
  17.6 5.0 %collective-permute-done.5 = f32[80,3,8,1]{0,2,3,1:T(8,128)S(1)} collective-permute-done((f32[80,3,8,1]{0,2,3,1:T(8,128)S(1)}, f32[80,3,8,1]{0,2,3,1:T(8,128)S(1)}, u32[]{:S(2)}, u32[]{:S(2)}) %collective-permute-start.5) | collective-permute-done | bytes 7712 | tf_op jit(solution)/shard_map/ppermute | solution.py:14
  24.8 112.4 %while.17 = (s32[]{:T(128)}, f32[80,3072]{1,0:T(8,128)S(1)}, s32[4,256]{1,0:T(4,128)}, s32[]{:T(128)}, s32[]{:T(128)}, /*index=5*/s32[]{:T(128)}, f32[4,256]{1,0...) while((s32[]{:T(128)}, f32[80,3072]{1,0:T(8,128)S(1)}, ...), condition=%wide.region_6.7_spmd.clone.clone, body=%wide.region_0.6_spmd.clone.clone.sunk | while | flops 1778674048 | bytes 35307480 | solution.py:99
  26.3 1.9 %collective-permute-start = (f32[80,256]{1,0:T(8,128)S(1)}, f32[80,256]{1,0:T(8,128)S(1)}, u32[]{:S(2)}, u32[]{:S(2)}) collective-permute-start(f32[80,256]{1,0:T(8,128)S(1)} %convolution_bitcast_fusion.2), channel_id=1, source_target_pairs={{32,0},{64,32},{96,64},{128,96},{160,128},{192,160},{224,192},{33,... | collective-permute-start | bytes 245768 | tf_op jit(solution)/shard_map/while/body/eval_jaxpr/ppermute | solution.py:14
  28.2 5.1 %collective-permute-start.1 = (f32[80,256]{1,0:T(8,128)S(1)}, f32[80,256]{1,0:T(8,128)S(1)}, u32[]{:S(2)}, u32[]{:S(2)}) collective-permute-start(f32[80,256]{1,0:T(8,128)S(1)} %convolution_bitcast_fusion.2), channel_id=1, source_target_pairs={{0,32},{32,64},{64,96},{96,128},{128,160},{160,192},{192,224},{1,3... | collective-permute-start | bytes 245768 | tf_op jit(solution)/shard_map/while/body/eval_jaxpr/ppermute | solution.py:14
  33.5 1.8 %select_reduce_fusion.4 = f32[256,128]{1,0:T(8,128)S(1)} fusion(f32[129]{0:T(256)S(1)} %get-tuple-element.544, s32[256,128]{1,0:T(8,128)S(1)} %subtract_minimum_fusion.2), kind=kLoop, calls=%fused_computation.2.clone.1 | loop fusion | flops 12648448 | bytes 262660 | tf_op jit(solution)/shard_map/while/body/eval_jaxpr/reduce_sum | solution.py:46
  38.7 2.4 %copy.41 = f32[256,3072]{1,0:T(8,128)} copy(f32[256,3072]{0,1:T(8,128)S(1)} %bitcast.41) | data formatting | bytes 6291456 | tf_op jit(solution)/shard_map/while/body/eval_jaxpr/tile | solution.py:96
  41.1 2.9 %collective-permute-done.3 = f32[80,256]{1,0:T(8,128)S(1)} collective-permute-done((f32[80,256]{1,0:T(8,128)S(1)}, f32[80,256]{1,0:T(8,128)S(1)}, u32[]{:S(2)}, u32[]{:S(2)}) %collective-permute-start.3) | collective-permute-done | bytes 81952 | tf_op jit(solution)/shard_map/while/body/eval_jaxpr/ppermute | solution.py:14
  44.8 5.1 %fusion.38 = f32[256,3072]{1,0:T(8,128)S(1)} fusion(f32[256,3072]{1,0:T(8,128)} %copy.41, f32[256]{0:T(256)S(1)} %multiply_add_fusion.3, f32[80,3072]{1,0:T(8,128)} %copy-done, f32[3072]{0:T(1024)S(1)} %broadcast_multiply_fusion.10, f32[80,256]{1,0:T(8,128)S(1)} %get-tuple-element.505, f32[256]{0:T(256)S(1)} %broadcast_multiply_fusion.9), kind=kOutput, calls=%fused_computation.7.clone.1 | convolution fusion | flops 757600256 | bytes 7370752 | tf_op jit(solution)/shard_map/while/body/eval_jaxpr/dot_general | solution.py:93
  50.0 2.2 %fusion.39 = (f32[3072]{0:T(1024)S(1)}, f32[80,3072]{1,0:T(8,128)S(1)}) fusion(f32[80,3072]{1,0:T(8,128)S(1)} %copy-done.1, f32[256,3072]{1,0:T(8,128)S(1)} %fusion.38, f32[80,256]{1,0:T(8,128)S(1)} %get-tuple-element.505, f32[256]{0:T(256)S(1)} %bitcast.50, f32[256]{0:T(256)S(1)} %bitcast.51, f32[256]{0:T(256)S(1)} %broadcast_multiply_fusion.9), kind=kOutput, calls=%fused_computation.70.clone.1 | convolution fusion | flops 755545088 | bytes 5209088 | tf_op jit(solution)/shard_map/while/body/eval_jaxpr/dot_general | solution.py:97
  53.5 1.9 %collective-permute-start = (f32[80,256]{1,0:T(8,128)S(1)}, f32[80,256]{1,0:T(8,128)S(1)}, u32[]{:S(2)}, u32[]{:S(2)}) collective-permute-start(f32[80,256]{1,0:T(8,128)S(1)} %convolution_bitcast_fusion.2), channel_id=1, source_target_pairs={{32,0},{64,32},{96,64},{128,96},{160,128},{192,160},{224,192},{33,... | collective-permute-start | bytes 245768 | tf_op jit(solution)/shard_map/while/body/eval_jaxpr/ppermute | solution.py:14
  55.5 5.1 %collective-permute-start.1 = (f32[80,256]{1,0:T(8,128)S(1)}, f32[80,256]{1,0:T(8,128)S(1)}, u32[]{:S(2)}, u32[]{:S(2)}) collective-permute-start(f32[80,256]{1,0:T(8,128)S(1)} %convolution_bitcast_fusion.2), channel_id=1, source_target_pairs={{0,32},{32,64},{64,96},{96,128},{128,160},{160,192},{192,224},{1,3... | collective-permute-start | bytes 245768 | tf_op jit(solution)/shard_map/while/body/eval_jaxpr/ppermute | solution.py:14
  66.6 2.4 %copy.41 = f32[256,3072]{1,0:T(8,128)} copy(f32[256,3072]{0,1:T(8,128)S(1)} %bitcast.41) | data formatting | bytes 6291456 | tf_op jit(solution)/shard_map/while/body/eval_jaxpr/tile | solution.py:96
  69.0 3.3 %collective-permute-done.3 = f32[80,256]{1,0:T(8,128)S(1)} collective-permute-done((f32[80,256]{1,0:T(8,128)S(1)}, f32[80,256]{1,0:T(8,128)S(1)}, u32[]{:S(2)}, u32[]{:S(2)}) %collective-permute-start.3) | collective-permute-done | bytes 81952 | tf_op jit(solution)/shard_map/while/body/eval_jaxpr/ppermute | solution.py:14
  73.2 5.1 %fusion.38 = f32[256,3072]{1,0:T(8,128)S(1)} fusion(f32[256,3072]{1,0:T(8,128)} %copy.41, f32[256]{0:T(256)S(1)} %multiply_add_fusion.3, f32[80,3072]{1,0:T(8,128)} %copy-done, f32[3072]{0:T(1024)S(1)} %broadcast_multiply_fusion.10, f32[80,256]{1,0:T(8,128)S(1)} %get-tuple-element.505, f32[256]{0:T(256)S(1)} %broadcast_multiply_fusion.9), kind=kOutput, calls=%fused_computation.7.clone.1 | convolution fusion | flops 757600256 | bytes 7370752 | tf_op jit(solution)/shard_map/while/body/eval_jaxpr/dot_general | solution.py:93
  78.3 2.2 %fusion.39 = (f32[3072]{0:T(1024)S(1)}, f32[80,3072]{1,0:T(8,128)S(1)}) fusion(f32[80,3072]{1,0:T(8,128)S(1)} %copy-done.1, f32[256,3072]{1,0:T(8,128)S(1)} %fusion.38, f32[80,256]{1,0:T(8,128)S(1)} %get-tuple-element.505, f32[256]{0:T(256)S(1)} %bitcast.50, f32[256]{0:T(256)S(1)} %bitcast.51, f32[256]{0:T(256)S(1)} %broadcast_multiply_fusion.9), kind=kOutput, calls=%fused_computation.70.clone.1 | convolution fusion | flops 755545088 | bytes 5209088 | tf_op jit(solution)/shard_map/while/body/eval_jaxpr/dot_general | solution.py:97
  81.8 1.9 %collective-permute-start = (f32[80,256]{1,0:T(8,128)S(1)}, f32[80,256]{1,0:T(8,128)S(1)}, u32[]{:S(2)}, u32[]{:S(2)}) collective-permute-start(f32[80,256]{1,0:T(8,128)S(1)} %convolution_bitcast_fusion.2), channel_id=1, source_target_pairs={{32,0},{64,32},{96,64},{128,96},{160,128},{192,160},{224,192},{33,... | collective-permute-start | bytes 245768 | tf_op jit(solution)/shard_map/while/body/eval_jaxpr/ppermute | solution.py:14
  83.8 5.1 %collective-permute-start.1 = (f32[80,256]{1,0:T(8,128)S(1)}, f32[80,256]{1,0:T(8,128)S(1)}, u32[]{:S(2)}, u32[]{:S(2)}) collective-permute-start(f32[80,256]{1,0:T(8,128)S(1)} %convolution_bitcast_fusion.2), channel_id=1, source_target_pairs={{0,32},{32,64},{64,96},{96,128},{128,160},{160,192},{192,224},{1,3... | collective-permute-start | bytes 245768 | tf_op jit(solution)/shard_map/while/body/eval_jaxpr/ppermute | solution.py:14
  94.9 2.4 %copy.41 = f32[256,3072]{1,0:T(8,128)} copy(f32[256,3072]{0,1:T(8,128)S(1)} %bitcast.41) | data formatting | bytes 6291456 | tf_op jit(solution)/shard_map/while/body/eval_jaxpr/tile | solution.py:96
  97.3 3.3 %collective-permute-done.3 = f32[80,256]{1,0:T(8,128)S(1)} collective-permute-done((f32[80,256]{1,0:T(8,128)S(1)}, f32[80,256]{1,0:T(8,128)S(1)}, u32[]{:S(2)}, u32[]{:S(2)}) %collective-permute-start.3) | collective-permute-done | bytes 81952 | tf_op jit(solution)/shard_map/while/body/eval_jaxpr/ppermute | solution.py:14
  101.5 5.1 %fusion.38 = f32[256,3072]{1,0:T(8,128)S(1)} fusion(f32[256,3072]{1,0:T(8,128)} %copy.41, f32[256]{0:T(256)S(1)} %multiply_add_fusion.3, f32[80,3072]{1,0:T(8,128)} %copy-done, f32[3072]{0:T(1024)S(1)} %broadcast_multiply_fusion.10, f32[80,256]{1,0:T(8,128)S(1)} %get-tuple-element.505, f32[256]{0:T(256)S(1)} %broadcast_multiply_fusion.9), kind=kOutput, calls=%fused_computation.7.clone.1 | convolution fusion | flops 757600256 | bytes 7370752 | tf_op jit(solution)/shard_map/while/body/eval_jaxpr/dot_general | solution.py:93
  106.6 2.2 %fusion.39 = (f32[3072]{0:T(1024)S(1)}, f32[80,3072]{1,0:T(8,128)S(1)}) fusion(f32[80,3072]{1,0:T(8,128)S(1)} %copy-done.1, f32[256,3072]{1,0:T(8,128)S(1)} %fusion.38, f32[80,256]{1,0:T(8,128)S(1)} %get-tuple-element.505, f32[256]{0:T(256)S(1)} %bitcast.50, f32[256]{0:T(256)S(1)} %bitcast.51, f32[256]{0:T(256)S(1)} %broadcast_multiply_fusion.9), kind=kOutput, calls=%fused_computation.70.clone.1 | convolution fusion | flops 755545088 | bytes 5209088 | tf_op jit(solution)/shard_map/while/body/eval_jaxpr/dot_general | solution.py:97
  110.2 1.9 %collective-permute-start = (f32[80,256]{1,0:T(8,128)S(1)}, f32[80,256]{1,0:T(8,128)S(1)}, u32[]{:S(2)}, u32[]{:S(2)}) collective-permute-start(f32[80,256]{1,0:T(8,128)S(1)} %convolution_bitcast_fusion.2), channel_id=1, source_target_pairs={{32,0},{64,32},{96,64},{128,96},{160,128},{192,160},{224,192},{33,... | collective-permute-start | bytes 245768 | tf_op jit(solution)/shard_map/while/body/eval_jaxpr/ppermute | solution.py:14
  112.1 5.1 %collective-permute-start.1 = (f32[80,256]{1,0:T(8,128)S(1)}, f32[80,256]{1,0:T(8,128)S(1)}, u32[]{:S(2)}, u32[]{:S(2)}) collective-permute-start(f32[80,256]{1,0:T(8,128)S(1)} %convolution_bitcast_fusion.2), channel_id=1, source_target_pairs={{0,32},{32,64},{64,96},{96,128},{128,160},{160,192},{192,224},{1,3... | collective-permute-start | bytes 245768 | tf_op jit(solution)/shard_map/while/body/eval_jaxpr/ppermute | solution.py:14
  123.2 2.4 %copy.41 = f32[256,3072]{1,0:T(8,128)} copy(f32[256,3072]{0,1:T(8,128)S(1)} %bitcast.41) | data formatting | bytes 6291456 | tf_op jit(solution)/shard_map/while/body/eval_jaxpr/tile | solution.py:96
  125.6 3.3 %collective-permute-done.3 = f32[80,256]{1,0:T(8,128)S(1)} collective-permute-done((f32[80,256]{1,0:T(8,128)S(1)}, f32[80,256]{1,0:T(8,128)S(1)}, u32[]{:S(2)}, u32[]{:S(2)}) %collective-permute-start.3) | collective-permute-done | bytes 81952 | tf_op jit(solution)/shard_map/while/body/eval_jaxpr/ppermute | solution.py:14
  129.8 5.1 %fusion.38 = f32[256,3072]{1,0:T(8,128)S(1)} fusion(f32[256,3072]{1,0:T(8,128)} %copy.41, f32[256]{0:T(256)S(1)} %multiply_add_fusion.3, f32[80,3072]{1,0:T(8,128)} %copy-done, f32[3072]{0:T(1024)S(1)} %broadcast_multiply_fusion.10, f32[80,256]{1,0:T(8,128)S(1)} %get-tuple-element.505, f32[256]{0:T(256)S(1)} %broadcast_multiply_fusion.9), kind=kOutput, calls=%fused_computation.7.clone.1 | convolution fusion | flops 757600256 | bytes 7370752 | tf_op jit(solution)/shard_map/while/body/eval_jaxpr/dot_general | solution.py:93
  134.9 2.2 %fusion.39 = (f32[3072]{0:T(1024)S(1)}, f32[80,3072]{1,0:T(8,128)S(1)}) fusion(f32[80,3072]{1,0:T(8,128)S(1)} %copy-done.1, f32[256,3072]{1,0:T(8,128)S(1)} %fusion.38, f32[80,256]{1,0:T(8,128)S(1)} %get-tuple-element.505, f32[256]{0:T(256)S(1)} %bitcast.50, f32[256]{0:T(256)S(1)} %bitcast.51, f32[256]{0:T(256)S(1)} %broadcast_multiply_fusion.9), kind=kOutput, calls=%fused_computation.70.clone.1 | convolution fusion | flops 755545088 | bytes 5209088 | tf_op jit(solution)/shard_map/while/body/eval_jaxpr/dot_general | solution.py:97
  (142 shorter events, 35.1 us)
Async XLA Ops:
  1.9 14.3 %copy-start.5 = (f32[8,128]{1,0:T(8,128)S(1)}, f32[8,128]{1,0:T(8,128)}, u32[]{:S(2)}) copy-start(f32[8,128]{1,0:T(8,128)} %param.12) | copy-start | bytes 12292
  2.0 14.3 %copy-start.6 = (f32[8,128]{1,0:T(8,128)S(1)}, f32[8,128]{1,0:T(8,128)}, u32[]{:S(2)}) copy-start(f32[8,128]{1,0:T(8,128)} %param.11) | copy-start | bytes 12292
  2.0 21.1 %collective-permute-start.6 = (f32[80,3,1,128]{3,0,2,1:T(8,128)S(1)}, f32[80,3,1,128]{3,0,2,1:T(8,128)S(1)}, u32[]{:S(2)}, u32[]{:S(2)}) collective-permute-start(f32[80,3,1,128]{3,0,2,1:T(8,128)S(1)} %copy.30), channel_id=1, source_target_pairs={{32,0},{64,32},{96,64},{128,96},{160,128},{192,160},{224,192},{33,... | collective-permute-start | bytes 368648 | tf_op jit(solution)/shard_map/ppermute | solution.py:14
  4.0 19.2 %collective-permute-start.7 = (f32[80,3,1,128]{3,0,2,1:T(8,128)S(1)}, f32[80,3,1,128]{3,0,2,1:T(8,128)S(1)}, u32[]{:S(2)}, u32[]{:S(2)}) collective-permute-start(f32[80,3,1,128]{3,0,2,1:T(8,128)S(1)} %copy.31), channel_id=1, source_target_pairs={{0,32},{32,64},{64,96},{96,128},{128,160},{160,192},{192,224},{1,3... | collective-permute-start | bytes 368648 | tf_op jit(solution)/shard_map/ppermute | solution.py:14
  11.1 12.2 %copy-start.2 = (f32[80,3,8,128]{3,2,1,0:T(8,128)S(1)}, f32[80,3,8,128]{3,2,1,0:T(8,128)}, u32[]{:S(2)}) copy-start(f32[80,3,8,128]{3,2,1,0:T(8,128)} %param.10) | copy-start | bytes 2949124
  11.5 5.7 %collective-permute-start.4 = (f32[80,3,8,1]{0,2,3,1:T(8,128)S(1)}, f32[80,3,8,1]{0,2,3,1:T(8,128)S(1)}, u32[]{:S(2)}, u32[]{:S(2)}) collective-permute-start(f32[80,3,8,1]{0,2,3,1:T(8,128)S(1)} %copy.28), channel_id=1, source_target_pairs={{0,31},{1,0},{2,1},{3,2},{4,3},{5,4},{6,5},{7,6},{8,7},{9,8},{10,9... | collective-permute-start | bytes 23048 | tf_op jit(solution)/shard_map/ppermute | solution.py:14
  16.2 6.5 %collective-permute-start.5 = (f32[80,3,8,1]{0,2,3,1:T(8,128)S(1)}, f32[80,3,8,1]{0,2,3,1:T(8,128)S(1)}, u32[]{:S(2)}, u32[]{:S(2)}) collective-permute-start(f32[80,3,8,1]{0,2,3,1:T(8,128)S(1)} %copy.29), channel_id=1, source_target_pairs={{0,1},{1,2},{2,3},{3,4},{4,5},{5,6},{6,7},{7,8},{8,9},{9,10},{10,1... | collective-permute-start | bytes 23048 | tf_op jit(solution)/shard_map/ppermute | solution.py:14
  23.4 1.4 %copy-start.3 = (f32[129]{0:T(256)S(1)}, f32[129]{0:T(256)}, u32[]{:S(2)}) copy-start(f32[129]{0:T(256)} %param.17) | copy-start | bytes 1552
  25.0 12.2 %copy-start = (f32[80,3072]{1,0:T(8,128)}, f32[80,3072]{1,0:T(8,128)S(1)}, u32[]{:S(2)}) copy-start(f32[80,3072]{1,0:T(8,128)S(1)} %get-tuple-element.524) | copy-start | bytes 2949124 | tf_op jit(solution)/shard_map/while
  26.3 10.3 %collective-permute-start = (f32[80,256]{1,0:T(8,128)S(1)}, f32[80,256]{1,0:T(8,128)S(1)}, u32[]{:S(2)}, u32[]{:S(2)}) collective-permute-start(f32[80,256]{1,0:T(8,128)S(1)} %convolution_bitcast_fusion.2), channel_id=1, source_target_pairs={{32,0},{64,32},{96,64},{128,96},{160,128},{192,160},{224,192},{33,... | collective-permute-start | bytes 245768 | tf_op jit(solution)/shard_map/while/body/eval_jaxpr/ppermute | solution.py:14
  28.2 8.4 %collective-permute-start.1 = (f32[80,256]{1,0:T(8,128)S(1)}, f32[80,256]{1,0:T(8,128)S(1)}, u32[]{:S(2)}, u32[]{:S(2)}) collective-permute-start(f32[80,256]{1,0:T(8,128)S(1)} %convolution_bitcast_fusion.2), channel_id=1, source_target_pairs={{0,32},{32,64},{64,96},{96,128},{128,160},{160,192},{192,224},{1,3... | collective-permute-start | bytes 245768 | tf_op jit(solution)/shard_map/while/body/eval_jaxpr/ppermute | solution.py:14
  36.6 4.4 %collective-permute-start.2 = (f32[80,256]{1,0:T(8,128)S(1)}, f32[80,256]{1,0:T(8,128)S(1)}, u32[]{:S(2)}, u32[]{:S(2)}) collective-permute-start(f32[80,256]{1,0:T(8,128)S(1)} %add_add_fusion.4), channel_id=1, source_target_pairs={{0,31},{1,0},{2,1},{3,2},{4,3},{5,4},{6,5},{7,6},{8,7},{9,8},{10,9... | collective-permute-start | bytes 245768 | tf_op jit(solution)/shard_map/while/body/eval_jaxpr/ppermute | solution.py:14
  36.7 7.3 %collective-permute-start.3 = (f32[80,256]{1,0:T(8,128)S(1)}, f32[80,256]{1,0:T(8,128)S(1)}, u32[]{:S(2)}, u32[]{:S(2)}) collective-permute-start(f32[80,256]{1,0:T(8,128)S(1)} %add_add_fusion.4), channel_id=1, source_target_pairs={{0,1},{1,2},{2,3},{3,4},{4,5},{5,6},{6,7},{7,8},{8,9},{9,10},{10,1... | collective-permute-start | bytes 245768 | tf_op jit(solution)/shard_map/while/body/eval_jaxpr/ppermute | solution.py:14
  44.8 5.2 %copy-start.1 = (f32[80,3072]{1,0:T(8,128)S(1)}, f32[80,3072]{1,0:T(8,128)}, u32[]{:S(2)}) copy-start(f32[80,3072]{1,0:T(8,128)} %copy-done) | copy-start | bytes 2949124 | tf_op jit(solution)/shard_map/while
  52.3 12.9 %copy-start = (f32[80,3072]{1,0:T(8,128)}, f32[80,3072]{1,0:T(8,128)S(1)}, u32[]{:S(2)}) copy-start(f32[80,3072]{1,0:T(8,128)S(1)} %get-tuple-element.524) | copy-start | bytes 2949124 | tf_op jit(solution)/shard_map/while
  53.5 10.3 %collective-permute-start = (f32[80,256]{1,0:T(8,128)S(1)}, f32[80,256]{1,0:T(8,128)S(1)}, u32[]{:S(2)}, u32[]{:S(2)}) collective-permute-start(f32[80,256]{1,0:T(8,128)S(1)} %convolution_bitcast_fusion.2), channel_id=1, source_target_pairs={{32,0},{64,32},{96,64},{128,96},{160,128},{192,160},{224,192},{33,... | collective-permute-start | bytes 245768 | tf_op jit(solution)/shard_map/while/body/eval_jaxpr/ppermute | solution.py:14
  55.5 8.4 %collective-permute-start.1 = (f32[80,256]{1,0:T(8,128)S(1)}, f32[80,256]{1,0:T(8,128)S(1)}, u32[]{:S(2)}, u32[]{:S(2)}) collective-permute-start(f32[80,256]{1,0:T(8,128)S(1)} %convolution_bitcast_fusion.2), channel_id=1, source_target_pairs={{0,32},{32,64},{64,96},{96,128},{128,160},{160,192},{192,224},{1,3... | collective-permute-start | bytes 245768 | tf_op jit(solution)/shard_map/while/body/eval_jaxpr/ppermute | solution.py:14
  63.9 5.1 %collective-permute-start.2 = (f32[80,256]{1,0:T(8,128)S(1)}, f32[80,256]{1,0:T(8,128)S(1)}, u32[]{:S(2)}, u32[]{:S(2)}) collective-permute-start(f32[80,256]{1,0:T(8,128)S(1)} %add_add_fusion.4), channel_id=1, source_target_pairs={{0,31},{1,0},{2,1},{3,2},{4,3},{5,4},{6,5},{7,6},{8,7},{9,8},{10,9... | collective-permute-start | bytes 245768 | tf_op jit(solution)/shard_map/while/body/eval_jaxpr/ppermute | solution.py:14
  65.1 7.2 %collective-permute-start.3 = (f32[80,256]{1,0:T(8,128)S(1)}, f32[80,256]{1,0:T(8,128)S(1)}, u32[]{:S(2)}, u32[]{:S(2)}) collective-permute-start(f32[80,256]{1,0:T(8,128)S(1)} %add_add_fusion.4), channel_id=1, source_target_pairs={{0,1},{1,2},{2,3},{3,4},{4,5},{5,6},{6,7},{7,8},{8,9},{9,10},{10,1... | collective-permute-start | bytes 245768 | tf_op jit(solution)/shard_map/while/body/eval_jaxpr/ppermute | solution.py:14
  73.1 5.2 %copy-start.1 = (f32[80,3072]{1,0:T(8,128)S(1)}, f32[80,3072]{1,0:T(8,128)}, u32[]{:S(2)}) copy-start(f32[80,3072]{1,0:T(8,128)} %copy-done) | copy-start | bytes 2949124 | tf_op jit(solution)/shard_map/while
  80.6 12.9 %copy-start = (f32[80,3072]{1,0:T(8,128)}, f32[80,3072]{1,0:T(8,128)S(1)}, u32[]{:S(2)}) copy-start(f32[80,3072]{1,0:T(8,128)S(1)} %get-tuple-element.524) | copy-start | bytes 2949124 | tf_op jit(solution)/shard_map/while
  81.8 10.3 %collective-permute-start = (f32[80,256]{1,0:T(8,128)S(1)}, f32[80,256]{1,0:T(8,128)S(1)}, u32[]{:S(2)}, u32[]{:S(2)}) collective-permute-start(f32[80,256]{1,0:T(8,128)S(1)} %convolution_bitcast_fusion.2), channel_id=1, source_target_pairs={{32,0},{64,32},{96,64},{128,96},{160,128},{192,160},{224,192},{33,... | collective-permute-start | bytes 245768 | tf_op jit(solution)/shard_map/while/body/eval_jaxpr/ppermute | solution.py:14
  83.8 8.4 %collective-permute-start.1 = (f32[80,256]{1,0:T(8,128)S(1)}, f32[80,256]{1,0:T(8,128)S(1)}, u32[]{:S(2)}, u32[]{:S(2)}) collective-permute-start(f32[80,256]{1,0:T(8,128)S(1)} %convolution_bitcast_fusion.2), channel_id=1, source_target_pairs={{0,32},{32,64},{64,96},{96,128},{128,160},{160,192},{192,224},{1,3... | collective-permute-start | bytes 245768 | tf_op jit(solution)/shard_map/while/body/eval_jaxpr/ppermute | solution.py:14
  92.2 5.1 %collective-permute-start.2 = (f32[80,256]{1,0:T(8,128)S(1)}, f32[80,256]{1,0:T(8,128)S(1)}, u32[]{:S(2)}, u32[]{:S(2)}) collective-permute-start(f32[80,256]{1,0:T(8,128)S(1)} %add_add_fusion.4), channel_id=1, source_target_pairs={{0,31},{1,0},{2,1},{3,2},{4,3},{5,4},{6,5},{7,6},{8,7},{9,8},{10,9... | collective-permute-start | bytes 245768 | tf_op jit(solution)/shard_map/while/body/eval_jaxpr/ppermute | solution.py:14
  93.4 7.2 %collective-permute-start.3 = (f32[80,256]{1,0:T(8,128)S(1)}, f32[80,256]{1,0:T(8,128)S(1)}, u32[]{:S(2)}, u32[]{:S(2)}) collective-permute-start(f32[80,256]{1,0:T(8,128)S(1)} %add_add_fusion.4), channel_id=1, source_target_pairs={{0,1},{1,2},{2,3},{3,4},{4,5},{5,6},{6,7},{7,8},{8,9},{9,10},{10,1... | collective-permute-start | bytes 245768 | tf_op jit(solution)/shard_map/while/body/eval_jaxpr/ppermute | solution.py:14
  101.5 5.2 %copy-start.1 = (f32[80,3072]{1,0:T(8,128)S(1)}, f32[80,3072]{1,0:T(8,128)}, u32[]{:S(2)}) copy-start(f32[80,3072]{1,0:T(8,128)} %copy-done) | copy-start | bytes 2949124 | tf_op jit(solution)/shard_map/while
  108.9 12.9 %copy-start = (f32[80,3072]{1,0:T(8,128)}, f32[80,3072]{1,0:T(8,128)S(1)}, u32[]{:S(2)}) copy-start(f32[80,3072]{1,0:T(8,128)S(1)} %get-tuple-element.524) | copy-start | bytes 2949124 | tf_op jit(solution)/shard_map/while
  110.2 10.3 %collective-permute-start = (f32[80,256]{1,0:T(8,128)S(1)}, f32[80,256]{1,0:T(8,128)S(1)}, u32[]{:S(2)}, u32[]{:S(2)}) collective-permute-start(f32[80,256]{1,0:T(8,128)S(1)} %convolution_bitcast_fusion.2), channel_id=1, source_target_pairs={{32,0},{64,32},{96,64},{128,96},{160,128},{192,160},{224,192},{33,... | collective-permute-start | bytes 245768 | tf_op jit(solution)/shard_map/while/body/eval_jaxpr/ppermute | solution.py:14
  112.1 8.4 %collective-permute-start.1 = (f32[80,256]{1,0:T(8,128)S(1)}, f32[80,256]{1,0:T(8,128)S(1)}, u32[]{:S(2)}, u32[]{:S(2)}) collective-permute-start(f32[80,256]{1,0:T(8,128)S(1)} %convolution_bitcast_fusion.2), channel_id=1, source_target_pairs={{0,32},{32,64},{64,96},{96,128},{128,160},{160,192},{192,224},{1,3... | collective-permute-start | bytes 245768 | tf_op jit(solution)/shard_map/while/body/eval_jaxpr/ppermute | solution.py:14
  120.5 5.1 %collective-permute-start.2 = (f32[80,256]{1,0:T(8,128)S(1)}, f32[80,256]{1,0:T(8,128)S(1)}, u32[]{:S(2)}, u32[]{:S(2)}) collective-permute-start(f32[80,256]{1,0:T(8,128)S(1)} %add_add_fusion.4), channel_id=1, source_target_pairs={{0,31},{1,0},{2,1},{3,2},{4,3},{5,4},{6,5},{7,6},{8,7},{9,8},{10,9... | collective-permute-start | bytes 245768 | tf_op jit(solution)/shard_map/while/body/eval_jaxpr/ppermute | solution.py:14
  121.7 7.2 %collective-permute-start.3 = (f32[80,256]{1,0:T(8,128)S(1)}, f32[80,256]{1,0:T(8,128)S(1)}, u32[]{:S(2)}, u32[]{:S(2)}) collective-permute-start(f32[80,256]{1,0:T(8,128)S(1)} %add_add_fusion.4), channel_id=1, source_target_pairs={{0,1},{1,2},{2,3},{3,4},{4,5},{5,6},{6,7},{7,8},{8,9},{9,10},{10,1... | collective-permute-start | bytes 245768 | tf_op jit(solution)/shard_map/while/body/eval_jaxpr/ppermute | solution.py:14
  129.8 5.2 %copy-start.1 = (f32[80,3072]{1,0:T(8,128)S(1)}, f32[80,3072]{1,0:T(8,128)}, u32[]{:S(2)}) copy-start(f32[80,3072]{1,0:T(8,128)} %copy-done) | copy-start | bytes 2949124 | tf_op jit(solution)/shard_map/while
  (1 other events, 1.4 us)

commit v2 on v1

--- a/solution.py
+++ b/solution.py
@@ -1,11 +1,20 @@
+import functools
 import jax
 import jax.numpy as jnp
 from jax import lax
+from jax.experimental import pallas as pl
+from jax.experimental.pallas import tpu as pltpu
 from jax.sharding import PartitionSpec as P
 
 diffusion_number = 0.2
 variance_eps = 1e-06
 highest = lax.Precision.HIGHEST
+mesh_ids = pl.DeviceIdType.MESH
+
+rows, cols, lats, lons = 8, 128, 8, 32
+members, channels, batches, batch_obs = 80, 3, 4, 256
+tile_room, room = 24, 24
+reach = 4
 
 
 def shifted(value, axis, by, closed):
@@ -23,7 +32,7 @@
     )
 
 
-def obs_increments(priors, values, error_var, members):
+def obs_increments(priors, values, error_var):
     prior_mean = jnp.mean(priors, axis=0)
     anomaly = priors - prior_mean
     variance = jnp.sum(anomaly * anomaly, axis=0) / (members - 1) + variance_eps
@@ -49,9 +58,9 @@
 def general(
     state, east_courant, north_courant, obs_cell, obs_value, obs_error_var, loc_lat, loc_lon
 ):
-    members, channels, tile_rows, tile_cols = state.shape
+    tile_rows, tile_cols = state.shape[2:]
     cell_count = tile_rows * tile_cols
-    batches, obs_count = obs_cell.shape
+    obs_count = obs_cell.shape[1]
     lat_padded = padded(state, "lat", 2, False)
     lon_padded = padded(state, "lon", 3, True)
     north_side = lat_padded[:, :, 2:, :]
@@ -88,7 +97,7 @@
         weights = (
             looked_up(loc_lat, lat_dist)[:, :, None] * looked_up(loc_lon, lon_dist)[:, None, :]
         ).reshape(obs_count, cell_count)
-        anomaly, variance, increments = obs_increments(priors, values, error_var, members)
+        anomaly, variance, increments = obs_increments(priors, values, error_var)
         field_anom = field - jnp.mean(field, axis=0)
         covar = lax.dot_general(
             anomaly, field_anom, (((0,), (0,)), ((), ())), precision=highest
@@ -98,6 +107,446 @@
 
     field = lax.fori_loop(0, batches, step, advected.reshape(members, channels * cell_count))
     return field.reshape(state.shape)
+
+
+def iota(shape, dim):
+    return lax.broadcasted_iota(jnp.int32, shape, dim)
+
+
+def one_hot(condition):
+    return condition.astype(jnp.float32)
+
+
+def dot_t(a, b, precision=None):
+    return lax.dot_general(
+        a, b, (((1,), (1,)), ((), ())), precision=precision, preferred_element_type=jnp.float32
+    )
+
+
+def earlier_counts(marks):
+    size = marks.shape[1]
+    earlier = (iota((size, size), 0) < iota((size, size), 1)).astype(jnp.bfloat16)
+    return jnp.dot(marks.astype(jnp.bfloat16), earlier, preferred_element_type=jnp.float32)
+
+
+def place(cells):
+    return cells >> 15, (cells >> 12) & 7, (cells >> 7) & 31, cells & 127
+
+
+def advect_row(here, north, south, west_halo, east_halo, east_courant, north_courant):
+    lane = iota(here.shape, 1)
+    east = jnp.where(lane == cols - 1, east_halo, pltpu.roll(here, cols - 1, 1))
+    west = jnp.where(lane == 0, west_halo, pltpu.roll(here, 1, 1))
+    return (
+        here
+        - 0.5 * east_courant * (east - west)
+        - 0.5 * north_courant * (north - south)
+        + diffusion_number * (east + west + north + south - 4.0 * here)
+    )
+
+
+def exchange_kernel(
+    state, east_courant, north_courant, obs_cell, adv_out, prior_out,
+    cells_in, from_north, from_south, edge_out, edge_in, lat_own, lat_in, col_own, lon_in,
+    load_sem, halo_send, halo_recv, lat_send, lat_recv, lon_send, lon_recv,
+):
+    la, lo = lax.axis_index("lat"), lax.axis_index("lon")
+
+    def at(dlat, dlon):
+        return ((la + dlat) & (lats - 1), (lo + dlon) & (lons - 1))
+
+    lat_steps = [1, 7, 2, 6, 3, 5, 4]
+    lon_steps = [1, -1, 2, -2, 3, -3, 4, -4]
+    barrier = pltpu.get_barrier_semaphore()
+    loads = [
+        [
+            pltpu.make_async_copy(
+                state.at[:, k, r, :], cells_in.at[k * rows + r], load_sem.at[k * rows + r]
+            )
+            for r in range(rows)
+        ]
+        for k in range(channels)
+    ]
+    for k in range(channels):
+        for load in loads[k]:
+            load.start()
+    peers = [at(1, 0), at(-1, 0), at(0, 1), at(0, -1)]
+    peers += [at(d, 0) for d in lat_steps[2:]] + [at(0, d) for d in lon_steps[2:]]
+    for peer in peers:
+        pl.semaphore_signal(barrier, inc=1, device_id=peer, device_id_type=mesh_ids)
+    lat_own[...] = jnp.zeros_like(lat_own)
+    lane = iota((members, cols), 1)
+
+    def pack_edges(k):
+        for side, column in ((0, 0), (1, cols - 1)):
+            packed = jnp.zeros((members, cols), jnp.float32)
+            for r in range(rows):
+                edge = cells_in[k * rows + r, :, column : column + 1]
+                packed = jnp.where(lane == r, edge, packed)
+            edge_out[side, k] = packed
+
+    def halo_copies(first, count, base):
+        made = []
+        sends = [
+            (cells_in.at[first * rows], from_north.at[first], at(-1, 0)),
+            (cells_in.at[first * rows + rows - 1], from_south.at[first], at(1, 0)),
+            (edge_out.at[1, first], edge_in.at[0, first], at(0, 1)),
+            (edge_out.at[0, first], edge_in.at[1, first], at(0, -1)),
+        ]
+        for i, (src, dst, peer) in enumerate(sends):
+            made.append(
+                pltpu.make_async_remote_copy(
+                    src_ref=src, dst_ref=dst, send_sem=halo_send.at[base + i],
+                    recv_sem=halo_recv.at[base + i], device_id=peer, device_id_type=mesh_ids,
+                )
+            )
+        return made
+
+    for load in loads[0]:
+        load.wait()
+    pack_edges(0)
+    pl.semaphore_wait(barrier, len(peers))
+    halos = [halo_copies(k, 1, 4 * k) for k in range(channels)]
+    for copy in halos[0]:
+        copy.start()
+    for k in range(1, channels):
+        for load in loads[k]:
+            load.wait()
+        pack_edges(k)
+        for copy in halos[k]:
+            copy.start()
+
+    lat_tile, row, lon_tile, col = place(obs_cell[...])
+    mine = [lon_tile[b : b + 1] == lo for b in range(batches)]
+    tile = (la - iota((lats, batch_obs), 0)) & (lats - 1)
+    marks = [one_hot((lat_tile[b : b + 1] == tile) & mine[b]) for b in range(batches)]
+    counts = earlier_counts(jnp.concatenate(marks, axis=0))
+    base = jnp.zeros((lats, 1), jnp.float32)
+    tile_slot, col_slot = [], []
+    for b in range(batches):
+        before = counts[b * lats : (b + 1) * lats]
+        tile_slot.append(jnp.where(marks[b] > 0, before + base, -1.0))
+        col_slot.append(jnp.where(mine[b], jnp.sum(before, axis=0, keepdims=True), -1.0))
+        base = base + jnp.sum(marks[b], axis=1, keepdims=True)
+    slot_ids = iota((tile_room, batch_obs), 0).astype(jnp.float32)
+    in_slot = [
+        [one_hot(tile_slot[b][d : d + 1] == slot_ids).astype(jnp.bfloat16) for d in range(lats)]
+        for b in range(batches)
+    ]
+    found = jnp.zeros((tile_room, 8), jnp.float32)
+    for b in range(batches):
+        kinds = iota((8, batch_obs), 0)
+        facts = jnp.where(
+            kinds == 0,
+            row[b : b + 1],
+            jnp.where(kinds == 1, col[b : b + 1], jnp.where(kinds == 2, 1, 0)),
+        ).astype(jnp.float32).astype(jnp.bfloat16)
+        found = found + dot_t(in_slot[b][0], facts)
+    slot_row = jnp.where(found[:, 2:3] > 0.5, found[:, 0:1], -1.0)
+    slot_col = found[:, 1:2]
+
+    def advect(k):
+        no_north, no_south = la == lats - 1, la == 0
+        for r in range(rows):
+            here = cells_in[k * rows + r]
+            if r + 1 < rows:
+                north = cells_in[k * rows + r + 1]
+            else:
+                north = jnp.where(no_north, 0.0, from_north[k])
+            if r > 0:
+                south = cells_in[k * rows + r - 1]
+            else:
+                south = jnp.where(no_south, 0.0, from_south[k])
+            adv_out[k * rows + r] = advect_row(
+                here, north, south, edge_in[0, k, :, r : r + 1], edge_in[1, k, :, r : r + 1],
+                east_courant[r : r + 1, :], north_courant[r : r + 1, :],
+            )
+
+    for copy in halos[0]:
+        copy.wait_recv()
+    advect(0)
+    spot = iota((tile_room, cols), 1).astype(jnp.float32)
+    picked = jnp.zeros((tile_room, members), jnp.float32)
+    for r in range(rows):
+        chosen = one_hot((slot_col == spot) & (slot_row == r))
+        picked = picked + dot_t(chosen, adv_out[r], highest)
+    lat_own[:, :members] = picked
+    lat_copies = []
+    for d in lat_steps:
+        copy = pltpu.make_async_remote_copy(
+            src_ref=lat_own, dst_ref=lat_in.at[d - 1], send_sem=lat_send.at[d - 1],
+            recv_sem=lat_recv.at[d - 1], device_id=at(d, 0), device_id_type=mesh_ids,
+        )
+        copy.start()
+        lat_copies.append(copy)
+
+    col_ids = iota((room, batch_obs), 0).astype(jnp.float32)
+    moves = []
+    for b in range(batches):
+        wanted = one_hot(col_slot[b] == col_ids).astype(jnp.bfloat16)
+        moves.append(dot_t(wanted, jnp.concatenate(in_slot[b], axis=0)))
+    move = jnp.concatenate(moves, axis=0)
+    for k in range(1, channels):
+        for copy in halos[k]:
+            copy.wait_recv()
+        advect(k)
+    for copy in lat_copies:
+        copy.wait_recv()
+    parts = jnp.concatenate([lat_own[...]] + [lat_in[d] for d in range(lats - 1)], axis=0)
+    column = jnp.dot(move, parts, precision=highest, preferred_element_type=jnp.float32)
+    col_own[...] = column
+    lon_copies = []
+    for i, d in enumerate(lon_steps):
+        size = room * (reach + 1 - abs(d))
+        size = min(size, room * batches)
+        copy = pltpu.make_async_remote_copy(
+            src_ref=col_own.at[pl.ds(0, size)], dst_ref=lon_in.at[reach - d, pl.ds(0, size)],
+            send_sem=lon_send.at[i], recv_sem=lon_recv.at[i],
+            device_id=at(0, d), device_id_type=mesh_ids,
+        )
+        copy.start()
+        lon_copies.append(copy)
+    prior_out[reach] = column
+    for i, d in enumerate(lon_steps):
+        lon_copies[i].wait_recv()
+    for d in lon_steps:
+        size = min(room * (reach + 1 - abs(d)), room * batches)
+        prior_out[reach - d, :size] = lon_in[reach - d, :size]
+        if size < room * batches:
+            prior_out[reach - d, size:] = jnp.zeros((room * batches - size, cols), jnp.float32)
+    for copies in (*halos, lat_copies, lon_copies):
+        for copy in copies:
+            copy.wait_send()
+
+
+def exchange(state, east_courant, north_courant, obs_cell):
+    vmem = pl.BlockSpec(memory_space=pltpu.VMEM)
+    f32 = jnp.float32
+    slots = room * batches
+    return pl.pallas_call(
+        exchange_kernel,
+        name="exchange",
+        out_shape=(
+            jax.ShapeDtypeStruct((channels * rows, members, cols), f32),
+            jax.ShapeDtypeStruct((2 * reach + 1, slots, cols), f32),
+        ),
+        in_specs=[pl.BlockSpec(memory_space=pl.ANY), vmem, vmem, vmem],
+        out_specs=(vmem, vmem),
+        scratch_shapes=[
+            pltpu.VMEM((channels * rows, members, cols), f32),
+            pltpu.VMEM((channels, members, cols), f32),
+            pltpu.VMEM((channels, members, cols), f32),
+            pltpu.VMEM((2, channels, members, cols), f32),
+            pltpu.VMEM((2, channels, members, cols), f32),
+            pltpu.VMEM((tile_room, cols), f32),
+            pltpu.VMEM((lats - 1, tile_room, cols), f32),
+            pltpu.VMEM((slots, cols), f32),
+            pltpu.VMEM((2 * reach + 1, slots, cols), f32),
+            pltpu.SemaphoreType.DMA((channels * rows,)),
+            pltpu.SemaphoreType.DMA((4 * channels,)),
+            pltpu.SemaphoreType.DMA((4 * channels,)),
+            pltpu.SemaphoreType.DMA((lats - 1,)),
+            pltpu.SemaphoreType.DMA((lats - 1,)),
+            pltpu.SemaphoreType.DMA((2 * reach,)),
+            pltpu.SemaphoreType.DMA((2 * reach,)),
+        ],
+        compiler_params=pltpu.CompilerParams(
+            collective_id=0, has_side_effects=True, vmem_limit_bytes=24 << 20
+        ),
+    )(state, east_courant, north_courant, obs_cell)
+
+
+def update_kernel(
+    adv, priors, obs_cell, obs_value, obs_error_var, loc_lat, loc_lon, out, field, slots, sem
+):
+    la, lo = lax.axis_index("lat"), lax.axis_index("lon")
+    lat_tile, row, lon_tile, col = place(obs_cell[...])
+    values, errors = obs_value[...], obs_error_var[...]
+    slots[...] = priors[...]
+
+    distance = jnp.abs(iota((cols * 2, 4 * cols), 1) - 2 * cols)
+    table = one_hot(distance == iota((cols * 2, 4 * cols), 0))
+    ends = one_hot(jnp.abs(iota((8, 4 * cols), 1) - 2 * cols) == cols)
+    line = jnp.dot(
+        jnp.broadcast_to(loc_lon[:, :cols], (8, cols)), table[:cols], precision=highest,
+        preferred_element_type=jnp.float32,
+    ) + ends * loc_lon[:, cols : cols + 1]
+    shifted_lines = pltpu.roll(
+        jnp.broadcast_to(line[0:1], (cols, 4 * cols)), 0, 1, stride=1, stride_axis=0
+    )
+    lon_table = shifted_lines[:, cols:]
+
+    def lat_weight(gap):
+        weight = jnp.zeros(gap.shape, jnp.float32)
+        for d in range(rows + 1):
+            weight = jnp.where(jnp.abs(gap) == d, loc_lat[d], weight)
+        return weight
+
+    lane = iota((1, cols), 1)
+    spans = [reach - b for b in range(batches)]
+    slot_ids = iota((room, batch_obs), 0).astype(jnp.float32)
+    col_of, row_of, value_of, error_of, lon_of, col_hot, row_hot, lat_of = ([] for _ in range(8))
+    tiles = (lo - reach + iota((16, batch_obs), 0)) & (lons - 1)
+    marks = [one_hot(lon_tile[b : b + 1] == tiles) for b in range(batches)]
+    counts = earlier_counts(jnp.concatenate(marks, axis=0))
+    for b in range(batches):
+        taken = jnp.where(marks[b] > 0, counts[16 * b : 16 * b + 16], -1.0)
+        hot = jnp.concatenate(
+            [
+                one_hot(taken[reach + k : reach + k + 1] == slot_ids)
+                for k in range(-spans[b], spans[b] + 1)
+            ],
+            axis=0,
+        )
+        kinds = iota((8, batch_obs), 0)
+        whole_row = (lat_tile[b : b + 1] * rows + row[b : b + 1]).astype(jnp.float32)
+        facts = jnp.where(kinds == 0, col[b : b + 1].astype(jnp.float32), 0.0)
+        facts = jnp.where(kinds == 1, whole_row, facts)
+        facts = jnp.where(kinds == 2, values[b : b + 1], facts)
+        facts = jnp.where(kinds == 3, errors[b : b + 1], facts)
+        facts = jnp.where(kinds == 4, 1.0, facts)
+        found = dot_t(hot, facts, highest)
+        valid = found[:, 4:5] > 0.5
+        where_col = jnp.where(valid, found[:, 0:1], -1.0).astype(jnp.int32)
+        where_row = found[:, 1:2].astype(jnp.int32)
+        value_of.append(found[:, 2:3])
+        error_of.append(jnp.where(valid, found[:, 3:4], 1.0))
+        row_of.append(where_row)
+        col_hot.append(one_hot(where_col == lane))
+        row_hot.append(one_hot(where_row == lane))
+        lon_of.append(
+            jnp.dot(
+                col_hot[b], lon_table, precision=highest, preferred_element_type=jnp.float32
+            )
+        )
+        lat_of.append(lat_weight(where_row - lane))
+
+    def block(b, k):
+        first = (k + spans[b]) * room
+        return slice(first, first + room)
+
+    def lon_field(b, k):
+        return jnp.concatenate(
+            [
+                lon_of[b][block(b, k - 1), 2 * cols : 3 * cols],
+                lon_of[b][block(b, k), cols : 2 * cols],
+                lon_of[b][block(b, k + 1), :cols],
+            ],
+            axis=0,
+        )
+
+    def around(k, b):
+        first = (k - 1 + spans[b]) * room
+        return slice(first, first + 3 * room)
+
+    later = {}
+    for b in range(batches - 1):
+        for k in range(-spans[b] + 1, spans[b]):
+            targets = [c for c in range(b + 1, batches) if abs(k) <= spans[c]]
+            cols_t = jnp.concatenate([col_hot[c][block(c, k)] for c in targets], axis=0)
+            rows_t = jnp.concatenate([row_hot[c][block(c, k)] for c in targets], axis=0)
+            later[b, k] = dot_t(lon_field(b, k), cols_t, highest) * dot_t(
+                lat_of[b][around(k, b)], rows_t, highest
+            )
+
+    is_member = lane < members
+    chunk = 4
+    copies = []
+    for b in range(batches):
+        mine = slice(b * room, (b + 1) * room)
+        prior = jnp.concatenate(
+            [slots[reach + k, mine] for k in range(-spans[b], spans[b] + 1)], axis=0
+        )
+        mean = jnp.sum(prior, axis=1, keepdims=True) / members
+        anomaly = jnp.where(is_member, prior - mean, 0.0)
+        variance = (
+            jnp.sum(anomaly * anomaly, axis=1, keepdims=True) / (members - 1) + variance_eps
+        )
+        post_var = 1.0 / (1.0 / variance + 1.0 / error_of[b])
+        post_mean = post_var * (mean / variance + value_of[b] / error_of[b])
+        increment = post_mean + jnp.sqrt(post_var / variance) * anomaly - prior
+        increment = jnp.where(is_member, increment, 0.0)
+        scaled = anomaly / ((members - 1) * variance)
+        for k in range(-spans[b] + 1, spans[b]):
+            if (b, k) not in later:
+                continue
+            first = (b + 1) * room
+            size = later[b, k].shape[1]
+            target = slots[reach + k, first : first + size]
+            gain = dot_t(scaled[around(k, b)], target, highest) * later[b, k]
+            slots[reach + k, first : first + size] = target + lax.dot_general(
+                gain, increment[around(k, b)], (((0,), (0,)), ((), ())), precision=highest,
+                preferred_element_type=jnp.float32,
+            )
+        near = around(0, b)
+        weights = lon_field(b, 0)
+        here_scaled, here_increment = scaled[near, :members], increment[near, :members]
+        by_row = [
+            lat_weight(row_of[b][near] - (la * rows + r)) * weights for r in range(rows)
+        ]
+        before = adv if b == 0 else field
+        for start in range(0, channels * rows, chunk):
+            cells = jnp.concatenate([before[start + i] for i in range(chunk)], axis=1)
+            covar = jnp.dot(
+                here_scaled, cells, precision=highest, preferred_element_type=jnp.float32
+            )
+            gain = covar * jnp.concatenate(
+                [by_row[(start + i) % rows] for i in range(chunk)], axis=1
+            )
+            cells = cells + lax.dot_general(
+                here_increment, gain, (((0,), (0,)), ((), ())), precision=highest,
+                preferred_element_type=jnp.float32,
+            )
+            for i in range(chunk):
+                field[start + i] = cells[:, i * cols : (i + 1) * cols]
+                if b == batches - 1:
+                    k, r = divmod(start + i, rows)
+                    copy = pltpu.make_async_copy(field.at[start + i], out.at[:, k, r, :], sem.at[start + i])
+                    copy.start()
+                    copies.append(copy)
+    for copy in copies:
+        copy.wait()
+
+
+def update(adv, priors, obs_cell, obs_value, obs_error_var, loc_lat, loc_lon):
+    vmem = pl.BlockSpec(memory_space=pltpu.VMEM)
+    smem = pl.BlockSpec(memory_space=pltpu.SMEM)
+    return pl.pallas_call(
+        update_kernel,
+        name="update",
+        out_shape=jax.ShapeDtypeStruct((members, channels, rows, cols), jnp.float32),
+        in_specs=[vmem] * 5 + [smem, vmem],
+        out_specs=pl.BlockSpec(memory_space=pl.ANY),
+        scratch_shapes=[
+            pltpu.VMEM((channels * rows, members, cols), jnp.float32),
+            pltpu.VMEM((2 * reach + 1, room * batches, cols), jnp.float32),
+            pltpu.SemaphoreType.DMA((channels * rows,)),
+        ],
+        compiler_params=pltpu.CompilerParams(vmem_limit_bytes=32 << 20),
+    )(adv, priors, obs_cell, obs_value, obs_error_var, loc_lat, loc_lon.reshape(1, -1))
+
+
+def fast(
+    state, east_courant, north_courant, obs_cell, obs_value, obs_error_var, loc_lat, loc_lon
+):
+    adv, priors = exchange(state, east_courant, north_courant, obs_cell)
+    return update(adv, priors, obs_cell, obs_value, obs_error_var, loc_lat, loc_lon)
+
+
+def fits(obs_cell):
+    lat_tile, _, lon_tile, _ = place(obs_cell)
+    tile = lat_tile * lons + lon_tile
+    in_tile = jnp.sum(
+        (tile.reshape(-1)[:, None] == jnp.arange(lats * lons)[None, :]).astype(jnp.int32), axis=0
+    )
+    in_column = jnp.sum(
+        (lon_tile[:, :, None] == jnp.arange(lons)[None, None, :]).astype(jnp.int32), axis=1
+    )
+    return (jnp.max(in_tile) <= tile_room) & (jnp.max(in_column) <= room)
+
+
+def on_device(*args):
+    return lax.cond(fits(args[3]), fast, general, *args)
 
 
 def solution(mesh):
@@ -113,5 +562,5 @@
     )
     out_specs = P(None, None, "lat", "lon")
     return jax.shard_map(
-        general, mesh=mesh, in_specs=in_specs, out_specs=out_specs, check_vma=False
-    )
+        on_device, mesh=mesh, in_specs=in_specs, out_specs=out_specs, check_vma=False
+    )

time: 139 us -> 55.5 us (0.40)
  the two profiles are of different devices: /device:TPU:96 before, /device:TPU:1 now
where the time goes in v2:
time: 55.5 us; the launch traced here: 55.3 us
  Pallas kernels  50.1 us (90%)
  other arithmetic  2.33 us (4%)
  between operations  1.33 us (2%)
  local copies, waits for them, and re-layouts  0.94 us (2%)
    pallas_call x1, Pallas kernels, exchange(): pl.pallas_call(exchange_kernel, name='exchange', out_shape=(jax.ShapeDtyp...  28.9 us
    pallas_call x1, Pallas kernels, update(): pl.pallas_call(update_kernel, name='update', out_shape=jax.ShapeDtypeStru...  21.2 us
    reduce_max x2, other arithmetic, fits(): return (jnp.max(in_tile) <= tile_room) & (jnp.max(in_column) <= room)  1.28 us

profile of v2, /device:TPU:1, one launch (start us, length us, event | category | flops | bytes accessed | tf_op | source)
XLA Modules:
  0.0 55.3 jit_solution(13093333346257105566)
XLA Ops:
  0.0 0.7 %shift-right-arithmetic_and_fusion = (s32[4,256]{1,0:T(4,128)S(1)}, s32[1,2,4,128]{3,2,1,0:T(4,128)S(1)}) fusion(s32[4,256]{1,0:T(4,128)} %param.15), kind=kLoop, calls=%fused_computation.74 | loop fusion | flops 5120 | bytes 12288 | tf_op jit(solution)/shard_map/and | solution.py:133
  0.7 0.2 convert_reduce_fusion
  0.9 0.6 %reduce_max.18 = s32[]{:T(128)} reduce(s32[256]{0:T(256)S(1)} %convert_reduce_fusion, s32[]{:T(128)} %constant.212.clone.1), dimensions={0}, to_apply=%region_1.0 | reduce | flops 255 | bytes 1032 | tf_op jit(solution)/shard_map/reduce_max | solution.py:545
  2.2 0.1 convert_reduce_fusion.1
  2.4 0.6 %reduce_max.19 = s32[]{:T(128)} reduce(s32[4,32]{1,0:T(4,128)S(1)} %convert_reduce_fusion.1, s32[]{:T(128)} %constant.212.clone.1), dimensions={0,1}, to_apply=%region_3.0 | reduce | flops 127 | bytes 520 | tf_op jit(solution)/shard_map/reduce_max | solution.py:545
  3.7 50.7 %conditional.1 = (f32[80,3,8,128]{3,2,1,0:T(8,128)S(1)}) conditional(s32[]{:T(128)} %convert_element_type.14, (f32[8,128]{1,0:T(8,128)}, f32[80,3,8,128]{3,2,1,0:T(8,128)}, f32[8,128]{1,0:T(8,128)}, s32[4,256]{1,0:T(4,128)}, f32[4,256]{1,0:T(4,128)}, /*index=5*/f32[4,256]{1,0:T(4,128)}, f32[9]{0:T(128)}, f32[129]{0:T(256)}) %tuple.33, ...), branch_computations={%region_4.12_spmd, %region_12.13_spmd} | conditional | flops 1783096704 | bytes 50050640 | solution.py:549
  3.9 28.9 %exchange.1 = (f32[24,80,128]{2,1,0:T(8,128)S(1)}, f32[9,96,128]{2,1,0:T(8,128)S(1)}) custom-call(f32[80,3,8,128]{3,2,1,0:T(8,128)} %get-tuple-element.321.state, f32[8,128]{1,0:T(8,128)} %get-tuple-element.322.east_courant, f32[8,128]{1,0:T(8,128)} %get-tuple-element.323.north_courant, s32[4,256]{1,0:T(4,128)} %get-tuple-element.324.obs_cell), custom_call_target="tpu_custom_call" | custom-call | tf_op jit(solution)/shard_map/cond/branch_1_fun/exchange/pallas_call | solution.py:326
  32.8 21.2 %update.1 = f32[80,3,8,128]{3,2,1,0:T(8,128)S(1)} custom-call(f32[24,80,128]{2,1,0:T(8,128)S(1)} %get-tuple-element.325.adv, f32[9,96,128]{2,1,0:T(8,128)S(1)} %get-tuple-element.326.priors, s32[4,256]{1,0:T(4,128)} %get-tuple-element.324.obs_cell, f32[4,256]{1,0:T(4,128)} %get-tuple-element.327.obs_value, f32[4,256]{1,0:T(4,128)} %get-tuple-element.328.obs_error_var, ...), custom_call_target="tpu_custom_call" | custom-call | tf_op jit(solution)/shard_map/cond/branch_1_fun/update/pallas_call | solution.py:514
  54.3 0.0 copy-start.2
  54.4 0.9 %copy-done.2 = f32[80,3,8,128]{3,2,1,0:T(8,128)} copy-done((f32[80,3,8,128]{3,2,1,0:T(8,128)}, f32[80,3,8,128]{3,2,1,0:T(8,128)S(1)}, u32[]{:S(2)}) %copy-start.2) | copy-done | bytes 983064
  (1 shorter events, 0.0 us)
Async XLA Ops:
  54.3 0.9 %copy-start.2 = (f32[80,3,8,128]{3,2,1,0:T(8,128)}, f32[80,3,8,128]{3,2,1,0:T(8,128)S(1)}, u32[]{:S(2)}) copy-start(f32[80,3,8,128]{3,2,1,0:T(8,128)S(1)} %get-tuple-element.642) | copy-start | bytes 2949124

commit v3 on v2

--- a/solution.py
+++ b/solution.py
@@ -123,6 +123,15 @@
     )
 
 
+def dot(a, b):
+    return jnp.dot(a, b, preferred_element_type=jnp.float32)
+
+
+def halves(value):
+    high = value.astype(jnp.bfloat16).astype(jnp.float32)
+    return high, value - high
+
+
 def earlier_counts(marks):
     size = marks.shape[1]
     earlier = (iota((size, size), 0) < iota((size, size), 1)).astype(jnp.bfloat16)
@@ -131,6 +140,61 @@
 
 def place(cells):
     return cells >> 15, (cells >> 12) & 7, (cells >> 7) & 31, cells & 127
+
+
+spans = [reach - b for b in range(batches)]
+
+
+def block(b, k):
+    first = (k + spans[b]) * room
+    return slice(first, first + room)
+
+
+def around(k, b):
+    first = (k - 1 + spans[b]) * room
+    return slice(first, first + 3 * room)
+
+
+def rows_of(b):
+    first = sum(2 * spans[c] + 1 for c in range(b)) * room
+    return slice(first, first + (2 * spans[b] + 1) * room)
+
+
+def targets(b):
+    return range(-spans[b] + 1, spans[b]) if b + 1 < batches else ()
+
+
+def later_batches(b, k):
+    return [c for c in range(b + 1, batches) if abs(k) <= spans[c]]
+
+
+def pair_rows(b, k):
+    return room * len(later_batches(b, k))
+
+
+pair_ids = {
+    pair: i for i, pair in enumerate((b, k) for b in range(batches) for k in targets(b))
+}
+
+
+def lat_weight(gap, loc_lat):
+    weight = jnp.zeros(gap.shape, jnp.float32)
+    for d in range(rows + 1):
+        weight = jnp.where(jnp.abs(gap) == d, loc_lat[d], weight)
+    return weight
+
+
+def column_weights(loc_lon):
+    wide = (2 * cols, 4 * cols)
+    distance = jnp.abs(iota(wide, 1) - 2 * cols)
+    table = one_hot(distance == iota(wide, 0))[:cols]
+    ends = one_hot(jnp.abs(iota((8, 4 * cols), 1) - 2 * cols) == cols)
+    line = jnp.dot(
+        jnp.broadcast_to(loc_lon[:, :cols], (8, cols)), table, precision=highest,
+        preferred_element_type=jnp.float32,
+    ) + ends * loc_lon[:, cols : cols + 1]
+    lines = jnp.broadcast_to(line[0:1], (cols, 4 * cols))
+    return pltpu.roll(lines, 0, 1, stride=1, stride_axis=0)[:, cols:]
 
 
 def advect_row(here, north, south, west_halo, east_halo, east_courant, north_courant):
@@ -146,7 +210,9 @@
 
 
 def exchange_kernel(
-    state, east_courant, north_courant, obs_cell, adv_out, prior_out,
+    state, east_courant_in, north_courant_in, obs_cell_in, obs_value_in, obs_error_var_in,
+    loc_lat, loc_lon_in, adv_out, prior_out, obs_terms, pair_weights, cell_weights, overflow,
+    east_courant, north_courant, obs_cell, obs_value, obs_error_var, loc_lon, small_sem,
     cells_in, from_north, from_south, edge_out, edge_in, lat_own, lat_in, col_own, lon_in,
     load_sem, halo_send, halo_recv, lat_send, lat_recv, lon_send, lon_recv,
 ):
@@ -167,9 +233,16 @@
         ]
         for k in range(channels)
     ]
-    for k in range(channels):
-        for load in loads[k]:
-            load.start()
+    pairs = [
+        (obs_cell_in, obs_cell), (east_courant_in, east_courant),
+        (north_courant_in, north_courant), (obs_value_in, obs_value),
+        (obs_error_var_in, obs_error_var), (loc_lon_in, loc_lon),
+    ]
+    small = [
+        pltpu.make_async_copy(src, dst, small_sem.at[i]) for i, (src, dst) in enumerate(pairs)
+    ]
+    for load in loads[0] + small + loads[1] + loads[2]:
+        load.start()
     peers = [at(1, 0), at(-1, 0), at(0, 1), at(0, -1)]
     peers += [at(d, 0) for d in lat_steps[2:]] + [at(0, d) for d in lon_steps[2:]]
     for peer in peers:
@@ -215,6 +288,9 @@
         pack_edges(k)
         for copy in halos[k]:
             copy.start()
+
+    for load in small:
+        load.wait()
 
     lat_tile, row, lon_tile, col = place(obs_cell[...])
     mine = [lon_tile[b : b + 1] == lo for b in range(batches)]
@@ -290,6 +366,58 @@
         for copy in halos[k]:
             copy.wait_recv()
         advect(k)
+
+    inverse_error = 1.0 / obs_error_var[...]
+    value_term = obs_value[...] * inverse_error
+    lon_table = column_weights(loc_lon)
+    lanes = iota((1, cols), 1)
+    tiles = (lo - reach + iota((16, batch_obs), 0)) & (lons - 1)
+    marks = [one_hot(lon_tile[b : b + 1] == tiles) for b in range(batches)]
+    counts = earlier_counts(jnp.concatenate(marks, axis=0))
+    row_ids, lon_of, col_hot, row_hot, lat_of = [], [], [], [], []
+    kinds = iota((8, batch_obs), 0)
+    for b in range(batches):
+        taken = jnp.where(marks[b] > 0, counts[16 * b : 16 * b + 16], -1.0)
+        hot = jnp.concatenate(
+            [
+                one_hot(taken[reach + k : reach + k + 1] == slot_ids)
+                for k in range(-spans[b], spans[b] + 1)
+            ],
+            axis=0,
+        )
+        one = slice(b, b + 1)
+        whole_row = (lat_tile[one] * rows + row[one]).astype(jnp.float32)
+        facts = jnp.where(kinds == 0, inverse_error[one], 0.0)
+        facts = jnp.where(kinds == 1, value_term[one], facts)
+        facts = jnp.where(kinds == 2, col[one].astype(jnp.float32), facts)
+        facts = jnp.where(kinds == 3, whole_row, facts)
+        facts = jnp.where(kinds == 4, 1.0, facts)
+        found = dot_t(hot, facts, highest)
+        obs_terms[rows_of(b), :] = found
+        at_col = jnp.where(found[:, 4:5] > 0.5, found[:, 2:3], -1.0).astype(jnp.int32)
+        at_row = found[:, 3:4].astype(jnp.int32)
+        row_ids.append(at_row)
+        col_hot.append(one_hot(at_col == lanes))
+        row_hot.append(one_hot(at_row == lanes))
+        lon_of.append(
+            jnp.dot(
+                col_hot[b], lon_table, precision=highest, preferred_element_type=jnp.float32
+            )
+        )
+        lat_of.append(lat_weight(at_row - lanes, loc_lat))
+
+    def lon_field(b, k):
+        return jnp.concatenate(
+            [
+                lon_of[b][block(b, k - 1), 2 * cols : 3 * cols],
+                lon_of[b][block(b, k), cols : 2 * cols],
+                lon_of[b][block(b, k + 1), :cols],
+            ],
+            axis=0,
+        )
+
+    unused = jnp.zeros((cols - 3 * room, cols), jnp.float32)
+
     for copy in lat_copies:
         copy.wait_recv()
     parts = jnp.concatenate([lat_own[...]] + [lat_in[d] for d in range(lats - 1)], axis=0)
@@ -307,6 +435,31 @@
         copy.start()
         lon_copies.append(copy)
     prior_out[reach] = column
+
+    for (b, k), i in pair_ids.items():
+        later = later_batches(b, k)
+        cols_t = jnp.concatenate([col_hot[c][block(c, k)] for c in later], axis=0)
+        rows_t = jnp.concatenate([row_hot[c][block(c, k)] for c in later], axis=0)
+        by_lon = jnp.concatenate([lon_field(b, k), unused], axis=0)
+        by_lat = jnp.concatenate([lat_of[b][around(k, b)], unused], axis=0)
+        pair_weights[i, : pair_rows(b, k)] = dot_t(cols_t, by_lon, highest) * dot_t(
+            rows_t, by_lat, highest
+        )
+    for b in range(batches):
+        weights = lon_field(b, 0)
+        for r in range(rows):
+            gap = row_ids[b][around(0, b)] - (la * rows + r)
+            cell_weights[b, r] = lat_weight(gap, loc_lat) * weights
+    in_tile = jnp.zeros((lats, lons), jnp.float32)
+    too_many = jnp.zeros((1, lons), jnp.float32)
+    for b in range(batches):
+        by_lat = one_hot(lat_tile[b : b + 1] == iota((lats, batch_obs), 0))
+        by_lon = one_hot(lon_tile[b : b + 1] == iota((lons, batch_obs), 0))
+        tally = dot_t(by_lat.astype(jnp.bfloat16), by_lon.astype(jnp.bfloat16))
+        in_tile = in_tile + tally
+        too_many = jnp.maximum(too_many, jnp.sum(tally, axis=0, keepdims=True) - room)
+    too_many = jnp.maximum(too_many, jnp.max(in_tile, axis=0, keepdims=True) - tile_room)
+    overflow[0, 0] = jnp.max(too_many).astype(jnp.int32)
     for i, d in enumerate(lon_steps):
         lon_copies[i].wait_recv()
     for d in lon_steps:
@@ -319,8 +472,11 @@
             copy.wait_send()
 
 
-def exchange(state, east_courant, north_courant, obs_cell):
+def exchange(
+    state, east_courant, north_courant, obs_cell, obs_value, obs_error_var, loc_lat, loc_lon
+):
     vmem = pl.BlockSpec(memory_space=pltpu.VMEM)
+    smem = pl.BlockSpec(memory_space=pltpu.SMEM)
     f32 = jnp.float32
     slots = room * batches
     return pl.pallas_call(
@@ -329,10 +485,21 @@
         out_shape=(
             jax.ShapeDtypeStruct((channels * rows, members, cols), f32),
             jax.ShapeDtypeStruct((2 * reach + 1, slots, cols), f32),
+            jax.ShapeDtypeStruct((rows_of(batches - 1).stop, 8), f32),
+            jax.ShapeDtypeStruct((len(pair_ids), 3 * room, cols), f32),
+            jax.ShapeDtypeStruct((batches, rows, 3 * room, cols), f32),
+            jax.ShapeDtypeStruct((1, 1), jnp.int32),
         ),
-        in_specs=[pl.BlockSpec(memory_space=pl.ANY), vmem, vmem, vmem],
-        out_specs=(vmem, vmem),
+        in_specs=[pl.BlockSpec(memory_space=pltpu.HBM)] * 6 + [smem, pl.BlockSpec(memory_space=pltpu.HBM)],
+        out_specs=(vmem,) * 5 + (smem,),
         scratch_shapes=[
+            pltpu.VMEM((rows, cols), f32),
+            pltpu.VMEM((rows, cols), f32),
+            pltpu.VMEM((batches, batch_obs), jnp.int32),
+            pltpu.VMEM((batches, batch_obs), f32),
+            pltpu.VMEM((batches, batch_obs), f32),
+            pltpu.VMEM((1, cols + 1), f32),
+            pltpu.SemaphoreType.DMA((6,)),
             pltpu.VMEM((channels * rows, members, cols), f32),
             pltpu.VMEM((channels, members, cols), f32),
             pltpu.VMEM((channels, members, cols), f32),
@@ -353,103 +520,18 @@
         compiler_params=pltpu.CompilerParams(
             collective_id=0, has_side_effects=True, vmem_limit_bytes=24 << 20
         ),
-    )(state, east_courant, north_courant, obs_cell)
-
-
-def update_kernel(
-    adv, priors, obs_cell, obs_value, obs_error_var, loc_lat, loc_lon, out, field, slots, sem
-):
-    la, lo = lax.axis_index("lat"), lax.axis_index("lon")
-    lat_tile, row, lon_tile, col = place(obs_cell[...])
-    values, errors = obs_value[...], obs_error_var[...]
+    )(
+        state, east_courant, north_courant, obs_cell, obs_value, obs_error_var, loc_lat,
+        loc_lon.reshape(1, -1),
+    )
+
+
+def update_kernel(adv, priors, obs_terms, pair_weights, cell_weights, out, field, slots, sem):
     slots[...] = priors[...]
-
-    distance = jnp.abs(iota((cols * 2, 4 * cols), 1) - 2 * cols)
-    table = one_hot(distance == iota((cols * 2, 4 * cols), 0))
-    ends = one_hot(jnp.abs(iota((8, 4 * cols), 1) - 2 * cols) == cols)
-    line = jnp.dot(
-        jnp.broadcast_to(loc_lon[:, :cols], (8, cols)), table[:cols], precision=highest,
-        preferred_element_type=jnp.float32,
-    ) + ends * loc_lon[:, cols : cols + 1]
-    shifted_lines = pltpu.roll(
-        jnp.broadcast_to(line[0:1], (cols, 4 * cols)), 0, 1, stride=1, stride_axis=0
-    )
-    lon_table = shifted_lines[:, cols:]
-
-    def lat_weight(gap):
-        weight = jnp.zeros(gap.shape, jnp.float32)
-        for d in range(rows + 1):
-            weight = jnp.where(jnp.abs(gap) == d, loc_lat[d], weight)
-        return weight
-
     lane = iota((1, cols), 1)
-    spans = [reach - b for b in range(batches)]
-    slot_ids = iota((room, batch_obs), 0).astype(jnp.float32)
-    col_of, row_of, value_of, error_of, lon_of, col_hot, row_hot, lat_of = ([] for _ in range(8))
-    tiles = (lo - reach + iota((16, batch_obs), 0)) & (lons - 1)
-    marks = [one_hot(lon_tile[b : b + 1] == tiles) for b in range(batches)]
-    counts = earlier_counts(jnp.concatenate(marks, axis=0))
-    for b in range(batches):
-        taken = jnp.where(marks[b] > 0, counts[16 * b : 16 * b + 16], -1.0)
-        hot = jnp.concatenate(
-            [
-                one_hot(taken[reach + k : reach + k + 1] == slot_ids)
-                for k in range(-spans[b], spans[b] + 1)
-            ],
-            axis=0,
-        )
-        kinds = iota((8, batch_obs), 0)
-        whole_row = (lat_tile[b : b + 1] * rows + row[b : b + 1]).astype(jnp.float32)
-        facts = jnp.where(kinds == 0, col[b : b + 1].astype(jnp.float32), 0.0)
-        facts = jnp.where(kinds == 1, whole_row, facts)
-        facts = jnp.where(kinds == 2, values[b : b + 1], facts)
-        facts = jnp.where(kinds == 3, errors[b : b + 1], facts)
-        facts = jnp.where(kinds == 4, 1.0, facts)
-        found = dot_t(hot, facts, highest)
-        valid = found[:, 4:5] > 0.5
-        where_col = jnp.where(valid, found[:, 0:1], -1.0).astype(jnp.int32)
-        where_row = found[:, 1:2].astype(jnp.int32)
-        value_of.append(found[:, 2:3])
-        error_of.append(jnp.where(valid, found[:, 3:4], 1.0))
-        row_of.append(where_row)
-        col_hot.append(one_hot(where_col == lane))
-        row_hot.append(one_hot(where_row == lane))
-        lon_of.append(
-            jnp.dot(
-                col_hot[b], lon_table, precision=highest, preferred_element_type=jnp.float32
-            )
-        )
-        lat_of.append(lat_weight(where_row - lane))
-
-    def block(b, k):
-        first = (k + spans[b]) * room
-        return slice(first, first + room)
-
-    def lon_field(b, k):
-        return jnp.concatenate(
-            [
-                lon_of[b][block(b, k - 1), 2 * cols : 3 * cols],
-                lon_of[b][block(b, k), cols : 2 * cols],
-                lon_of[b][block(b, k + 1), :cols],
-            ],
-            axis=0,
-        )
-
-    def around(k, b):
-        first = (k - 1 + spans[b]) * room
-        return slice(first, first + 3 * room)
-
-    later = {}
-    for b in range(batches - 1):
-        for k in range(-spans[b] + 1, spans[b]):
-            targets = [c for c in range(b + 1, batches) if abs(k) <= spans[c]]
-            cols_t = jnp.concatenate([col_hot[c][block(c, k)] for c in targets], axis=0)
-            rows_t = jnp.concatenate([row_hot[c][block(c, k)] for c in targets], axis=0)
-            later[b, k] = dot_t(lon_field(b, k), cols_t, highest) * dot_t(
-                lat_of[b][around(k, b)], rows_t, highest
-            )
-
     is_member = lane < members
+    unused = jnp.zeros((cols - 3 * room, cols), jnp.float32)
+    unused_three = jnp.zeros((cols - 3 * room, 3 * cols), jnp.float32)
     chunk = 4
     copies = []
     for b in range(batches):
@@ -462,91 +544,105 @@
         variance = (
             jnp.sum(anomaly * anomaly, axis=1, keepdims=True) / (members - 1) + variance_eps
         )
-        post_var = 1.0 / (1.0 / variance + 1.0 / error_of[b])
-        post_mean = post_var * (mean / variance + value_of[b] / error_of[b])
-        increment = post_mean + jnp.sqrt(post_var / variance) * anomaly - prior
+        precision = 1.0 / variance
+        post_var = 1.0 / (precision + obs_terms[rows_of(b), 0:1])
+        post_mean = post_var * (mean * precision + obs_terms[rows_of(b), 1:2])
+        increment = post_mean + jnp.sqrt(post_var * precision) * anomaly - prior
         increment = jnp.where(is_member, increment, 0.0)
-        scaled = anomaly / ((members - 1) * variance)
-        for k in range(-spans[b] + 1, spans[b]):
-            if (b, k) not in later:
-                continue
+        scaled = anomaly * (precision / (members - 1))
+        increment_high, increment_low = halves(increment)
+        scaled_high, scaled_low = halves(scaled)
+        scaled_three = jnp.concatenate([scaled_high, scaled_high, scaled_low], axis=1)
+        for k in targets(b):
             first = (b + 1) * room
-            size = later[b, k].shape[1]
+            size = pair_rows(b, k)
             target = slots[reach + k, first : first + size]
-            gain = dot_t(scaled[around(k, b)], target, highest) * later[b, k]
-            slots[reach + k, first : first + size] = target + lax.dot_general(
-                gain, increment[around(k, b)], (((0,), (0,)), ((), ())), precision=highest,
-                preferred_element_type=jnp.float32,
+            high, low = halves(target)
+            target_three = jnp.concatenate([high, low, high], axis=1).astype(jnp.bfloat16)
+            sources = jnp.concatenate([scaled_three[around(k, b)], unused_three], axis=0)
+            gain = dot_t(target_three, sources.astype(jnp.bfloat16))
+            high, low = halves(gain * pair_weights[pair_ids[b, k], :size])
+            gain_three = jnp.concatenate([high, low, high], axis=1).astype(jnp.bfloat16)
+            near_high = jnp.concatenate([increment_high[around(k, b)], unused], axis=0)
+            near_low = jnp.concatenate([increment_low[around(k, b)], unused], axis=0)
+            near_three = jnp.concatenate([near_high, near_high, near_low], axis=0)
+            slots[reach + k, first : first + size] = target + dot(
+                gain_three, near_three.astype(jnp.bfloat16)
             )
         near = around(0, b)
-        weights = lon_field(b, 0)
-        here_scaled, here_increment = scaled[near, :members], increment[near, :members]
-        by_row = [
-            lat_weight(row_of[b][near] - (la * rows + r)) * weights for r in range(rows)
-        ]
+        none = jnp.zeros((3 * room, cols), jnp.float32)
+        high = jnp.concatenate([scaled_high[near], none], axis=1)
+        low = jnp.concatenate([scaled_low[near], none], axis=1)
+        scaled_by_member = (
+            high + pltpu.roll(high, members, 1) + pltpu.roll(low, 2 * members, 1)
+        ).astype(jnp.bfloat16)
+        increment_by_slot = jnp.concatenate(
+            [
+                increment_high[near],
+                increment_high[near],
+                increment_low[near],
+                jnp.zeros((2 * cols - 9 * room, cols), jnp.float32),
+            ],
+            axis=0,
+        )
+        increment_by_slot = increment_by_slot.T[:members].astype(jnp.bfloat16)
         before = adv if b == 0 else field
         for start in range(0, channels * rows, chunk):
             cells = jnp.concatenate([before[start + i] for i in range(chunk)], axis=1)
-            covar = jnp.dot(
-                here_scaled, cells, precision=highest, preferred_element_type=jnp.float32
+            high = cells.astype(jnp.bfloat16)
+            low = (cells - high.astype(jnp.float32)).astype(jnp.bfloat16)
+            three = jnp.concatenate(
+                [high, low, high, jnp.zeros((2 * cols - 3 * members, chunk * cols), jnp.bfloat16)],
+                axis=0,
             )
-            gain = covar * jnp.concatenate(
-                [by_row[(start + i) % rows] for i in range(chunk)], axis=1
+            gain = dot(scaled_by_member, three) * jnp.concatenate(
+                [cell_weights[b, (start + i) % rows] for i in range(chunk)], axis=1
             )
-            cells = cells + lax.dot_general(
-                here_increment, gain, (((0,), (0,)), ((), ())), precision=highest,
-                preferred_element_type=jnp.float32,
-            )
+            high, low = halves(gain)
+            three = jnp.concatenate(
+                [high, low, high, jnp.zeros((2 * cols - 9 * room, chunk * cols), jnp.float32)],
+                axis=0,
+            ).astype(jnp.bfloat16)
+            cells = cells + dot(increment_by_slot, three)
             for i in range(chunk):
                 field[start + i] = cells[:, i * cols : (i + 1) * cols]
                 if b == batches - 1:
                     k, r = divmod(start + i, rows)
-                    copy = pltpu.make_async_copy(field.at[start + i], out.at[:, k, r, :], sem.at[start + i])
+                    copy = pltpu.make_async_copy(
+                        field.at[start + i], out.at[:, k, r, :], sem.at[start + i]
+                    )
                     copy.start()
                     copies.append(copy)
     for copy in copies:
         copy.wait()
 
 
-def update(adv, priors, obs_cell, obs_value, obs_error_var, loc_lat, loc_lon):
+def update(*operands):
     vmem = pl.BlockSpec(memory_space=pltpu.VMEM)
-    smem = pl.BlockSpec(memory_space=pltpu.SMEM)
     return pl.pallas_call(
         update_kernel,
         name="update",
         out_shape=jax.ShapeDtypeStruct((members, channels, rows, cols), jnp.float32),
-        in_specs=[vmem] * 5 + [smem, vmem],
-        out_specs=pl.BlockSpec(memory_space=pl.ANY),
+        in_specs=[vmem] * 5,
+        out_specs=pl.BlockSpec(memory_space=pltpu.HBM),
         scratch_shapes=[
             pltpu.VMEM((channels * rows, members, cols), jnp.float32),
             pltpu.VMEM((2 * reach + 1, room * batches, cols), jnp.float32),
             pltpu.SemaphoreType.DMA((channels * rows,)),
         ],
         compiler_params=pltpu.CompilerParams(vmem_limit_bytes=32 << 20),
-    )(adv, priors, obs_cell, obs_value, obs_error_var, loc_lat, loc_lon.reshape(1, -1))
-
-
-def fast(
-    state, east_courant, north_courant, obs_cell, obs_value, obs_error_var, loc_lat, loc_lon
-):
-    adv, priors = exchange(state, east_courant, north_courant, obs_cell)
-    return update(adv, priors, obs_cell, obs_value, obs_error_var, loc_lat, loc_lon)
-
-
-def fits(obs_cell):
-    lat_tile, _, lon_tile, _ = place(obs_cell)
-    tile = lat_tile * lons + lon_tile
-    in_tile = jnp.sum(
-        (tile.reshape(-1)[:, None] == jnp.arange(lats * lons)[None, :]).astype(jnp.int32), axis=0
-    )
-    in_column = jnp.sum(
-        (lon_tile[:, :, None] == jnp.arange(lons)[None, None, :]).astype(jnp.int32), axis=1
-    )
-    return (jnp.max(in_tile) <= tile_room) & (jnp.max(in_column) <= room)
+    )(*operands)
 
 
 def on_device(*args):
-    return lax.cond(fits(args[3]), fast, general, *args)
+    *operands, overflow = exchange(*args)
+    return lax.cond(
+        overflow.reshape(()) > 0,
+        lambda args, operands: general(*args),
+        lambda args, operands: update(*operands),
+        args,
+        tuple(operands),
+    )
 
 
 def solution(mesh):

time: 55.5 us -> 40.6 us (0.73)
  Pallas kernels: 50.1 us -> 38.6 us
  other arithmetic: 2.33 us -> 0 us
  between operations: 1.33 us -> 0.65 us
    pallas_call x1, Pallas kernels: 21.2 us -> 8.98 us  [update(): pl.pallas_call(update_kernel, name='update', out_shape=jax.ShapeDtypeStru...]
    reduce_max x2 -> x0, other arithmetic: 1.28 us -> none  [fits(): return (jnp.max(in_tile) <= tile_room) & (jnp.max(in_column) <= room)]
    pallas_call x1, Pallas kernels: 28.9 us -> 29.6 us  [exchange(): pl.pallas_call(exchange_kernel, name='exchange', out_shape=(jax.ShapeDtyp...]
    and x1 -> x0, other arithmetic: 0.69 us -> none  [place(): return (cells >> 15, cells >> 12 & 7, cells >> 7 & 31, cells & 127)]
where the time goes in v3:
time: 40.6 us; the launch traced here: 40.4 us
  Pallas kernels  38.6 us (95%)
  local copies, waits for them, and re-layouts  0.94 us (2%)
  between operations  0.65 us (2%)
    pallas_call x1, Pallas kernels, exchange(): pl.pallas_call(exchange_kernel, name='exchange', out_shape=(jax.ShapeDtyp...  29.6 us
    pallas_call x1, Pallas kernels, update(): pl.pallas_call(update_kernel, name='update', out_shape=jax.ShapeDtypeStru...  8.98 us
    unnamed x2, local copies, waits for them, and re-layouts  0.94 us

profile of v3, /device:TPU:1, one launch (start us, length us, event | category | flops | bytes accessed | tf_op | source)
XLA Modules:
  0.0 40.4 jit_solution(4239599750415321105)
XLA Ops:
  0.0 29.6 %exchange.1 = (f32[24,80,128]{2,1,0:T(8,128)S(1)}, f32[9,96,128]{2,1,0:T(8,128)S(1)}, f32[576,8]{1,0:T(8,128)S(1)}, f32[15,72,128]{2,1,0:T(8,128)S(1)}, f32[4,8,72,128]{3,2,1,0:T(8,128)S(1)}, /*index=5*/s32[1,1]{1,0:T(1,128)}) custom-call(f32[80,3,8,128]{3,2,1,0:T(8,128)} %state.1, f32[8,128]{1,0:T(8,128)} %east_courant_in.1, f32[8,128]{1,0:T(8,128)} %north_courant_in.1, ...), custom_call_target="tpu_custom_call" | custom-call | tf_op jit(solution)/shard_map/exchange/pallas_call | solution.py:482
  30.3 9.2 %conditional.1 = (f32[80,3,8,128]{3,2,1,0:T(8,128)S(1)}) conditional(s32[]{:T(128)} %bitcast.1, (f32[24,80,128]{2,1,0:T(8,128)S(1)}, f32[9,96,128]{2,1,0:T(8,128)S(1)}, f32[576,8]{1,0:T(8,128)S(1)}, f32[15,72,128]{2,1,0:T(8,128)S(1)}, f32[4,8,72,128]{3,2,1,0:T(8,128)S(1)}) %tuple.33, (f32[8,128]{1,0:T(8,128)}, f32[80,3,8,128]{3,2,1,0:T(8,128)}, ...), branch_computations={%region_0.0_spmd, %region_1.9_spmd} | conditional | flops 1783096704 | bytes 50050640 | solution.py:639
  30.5 9.0 %update.1 = f32[80,3,8,128]{3,2,1,0:T(8,128)S(1)} custom-call(f32[24,80,128]{2,1,0:T(8,128)S(1)} %get-tuple-element.293.adv, f32[9,96,128]{2,1,0:T(8,128)S(1)} %get-tuple-element.294.priors, f32[576,8]{1,0:T(8,128)S(1)} %get-tuple-element.295.obs_terms, f32[15,72,128]{2,1,0:T(8,128)S(1)} %get-tuple-element.296.pair_weights, ...), custom_call_target="tpu_custom_call" | custom-call | tf_op jit(solution)/shard_map/cond/branch_0_fun/update/pallas_call | solution.py:622
  39.5 0.0 copy-start.2
  39.5 0.9 %copy-done.2 = f32[80,3,8,128]{3,2,1,0:T(8,128)} copy-done((f32[80,3,8,128]{3,2,1,0:T(8,128)}, f32[80,3,8,128]{3,2,1,0:T(8,128)S(1)}, u32[]{:S(2)}) %copy-start.2) | copy-done | bytes 983064
Async XLA Ops:
  39.5 0.9 %copy-start.2 = (f32[80,3,8,128]{3,2,1,0:T(8,128)}, f32[80,3,8,128]{3,2,1,0:T(8,128)S(1)}, u32[]{:S(2)}) copy-start(f32[80,3,8,128]{3,2,1,0:T(8,128)S(1)} %get-tuple-element.641) | copy-start | bytes 2949124

commit v4 on v3

--- a/solution.py
+++ b/solution.py
@@ -13,7 +13,7 @@
 
 rows, cols, lats, lons = 8, 128, 8, 32
 members, channels, batches, batch_obs = 80, 3, 4, 256
-tile_room, room = 24, 24
+tile_room, room, packed_room = 24, 24, 16
 reach = 4
 
 
@@ -197,6 +197,26 @@
     return pltpu.roll(lines, 0, 1, stride=1, stride_axis=0)[:, cols:]
 
 
+def packed(block):
+    lane = iota((8, cols), 1)
+    last = block[16:24]
+    return jnp.concatenate(
+        [
+            jnp.where(lane < members, block[:8], pltpu.roll(last, members, 1)),
+            jnp.where(lane < members, block[8:16], pltpu.roll(last, 32, 1)),
+        ],
+        axis=0,
+    )
+
+
+def unpacked(block):
+    lane = iota((8, cols), 1)
+    first, second = block[:8], block[8:16]
+    last = jnp.where(lane < 48, pltpu.roll(first, 48, 1), pltpu.roll(second, 96, 1))
+    three = [jnp.where(lane < members, part, 0.0) for part in (first, second, last)]
+    return jnp.concatenate(three, axis=0)
+
+
 def advect_row(here, north, south, west_halo, east_halo, east_courant, north_courant):
     lane = iota(here.shape, 1)
     east = jnp.where(lane == cols - 1, east_halo, pltpu.roll(here, cols - 1, 1))
@@ -213,7 +233,7 @@
     state, east_courant_in, north_courant_in, obs_cell_in, obs_value_in, obs_error_var_in,
     loc_lat, loc_lon_in, adv_out, prior_out, obs_terms, pair_weights, cell_weights, overflow,
     east_courant, north_courant, obs_cell, obs_value, obs_error_var, loc_lon, small_sem,
-    cells_in, from_north, from_south, edge_out, edge_in, lat_own, lat_in, col_own, lon_in,
+    cells_in, from_north, from_south, edge_out, edge_in, lat_own, lat_in, lon_in,
     load_sem, halo_send, halo_recv, lat_send, lat_recv, lon_send, lon_recv,
 ):
     la, lo = lax.axis_index("lat"), lax.axis_index("lon")
@@ -221,8 +241,12 @@
     def at(dlat, dlon):
         return ((la + dlat) & (lats - 1), (lo + dlon) & (lons - 1))
 
-    lat_steps = [1, 7, 2, 6, 3, 5, 4]
-    lon_steps = [1, -1, 2, -2, 3, -3, 4, -4]
+    lat_steps = [4, 3, 5, 2, 6, 1, 7]
+    lon_steps = [4, -4, 3, -3, 2, -2, 1, -1]
+
+    def prior_rows(d):
+        return packed_room * min(reach + 1 - abs(d), batches)
+
     barrier = pltpu.get_barrier_semaphore()
     loads = [
         [
@@ -244,10 +268,13 @@
     for load in loads[0] + small + loads[1] + loads[2]:
         load.start()
     peers = [at(1, 0), at(-1, 0), at(0, 1), at(0, -1)]
-    peers += [at(d, 0) for d in lat_steps[2:]] + [at(0, d) for d in lon_steps[2:]]
+    peers += [at(d, 0) for d in lat_steps[:-2]] + [at(0, d) for d in lon_steps[:-2]]
     for peer in peers:
         pl.semaphore_signal(barrier, inc=1, device_id=peer, device_id_type=mesh_ids)
-    lat_own[...] = jnp.zeros_like(lat_own)
+    for d in lon_steps:
+        unsent = packed_room * batches - prior_rows(d)
+        if unsent:
+            lon_in[reach - d, prior_rows(d) :] = jnp.zeros((unsent, cols), jnp.float32)
     lane = iota((members, cols), 1)
 
     def pack_edges(k):
@@ -282,12 +309,6 @@
     halos = [halo_copies(k, 1, 4 * k) for k in range(channels)]
     for copy in halos[0]:
         copy.start()
-    for k in range(1, channels):
-        for load in loads[k]:
-            load.wait()
-        pack_edges(k)
-        for copy in halos[k]:
-            copy.start()
 
     for load in small:
         load.wait()
@@ -321,51 +342,12 @@
     slot_row = jnp.where(found[:, 2:3] > 0.5, found[:, 0:1], -1.0)
     slot_col = found[:, 1:2]
 
-    def advect(k):
-        no_north, no_south = la == lats - 1, la == 0
-        for r in range(rows):
-            here = cells_in[k * rows + r]
-            if r + 1 < rows:
-                north = cells_in[k * rows + r + 1]
-            else:
-                north = jnp.where(no_north, 0.0, from_north[k])
-            if r > 0:
-                south = cells_in[k * rows + r - 1]
-            else:
-                south = jnp.where(no_south, 0.0, from_south[k])
-            adv_out[k * rows + r] = advect_row(
-                here, north, south, edge_in[0, k, :, r : r + 1], edge_in[1, k, :, r : r + 1],
-                east_courant[r : r + 1, :], north_courant[r : r + 1, :],
-            )
-
-    for copy in halos[0]:
-        copy.wait_recv()
-    advect(0)
-    spot = iota((tile_room, cols), 1).astype(jnp.float32)
-    picked = jnp.zeros((tile_room, members), jnp.float32)
-    for r in range(rows):
-        chosen = one_hot((slot_col == spot) & (slot_row == r))
-        picked = picked + dot_t(chosen, adv_out[r], highest)
-    lat_own[:, :members] = picked
-    lat_copies = []
-    for d in lat_steps:
-        copy = pltpu.make_async_remote_copy(
-            src_ref=lat_own, dst_ref=lat_in.at[d - 1], send_sem=lat_send.at[d - 1],
-            recv_sem=lat_recv.at[d - 1], device_id=at(d, 0), device_id_type=mesh_ids,
-        )
-        copy.start()
-        lat_copies.append(copy)
-
     col_ids = iota((room, batch_obs), 0).astype(jnp.float32)
     moves = []
     for b in range(batches):
         wanted = one_hot(col_slot[b] == col_ids).astype(jnp.bfloat16)
         moves.append(dot_t(wanted, jnp.concatenate(in_slot[b], axis=0)))
     move = jnp.concatenate(moves, axis=0)
-    for k in range(1, channels):
-        for copy in halos[k]:
-            copy.wait_recv()
-        advect(k)
 
     inverse_error = 1.0 / obs_error_var[...]
     value_term = obs_value[...] * inverse_error
@@ -376,7 +358,8 @@
     counts = earlier_counts(jnp.concatenate(marks, axis=0))
     row_ids, lon_of, col_hot, row_hot, lat_of = [], [], [], [], []
     kinds = iota((8, batch_obs), 0)
-    for b in range(batches):
+
+    def describe(b):
         taken = jnp.where(marks[b] > 0, counts[16 * b : 16 * b + 16], -1.0)
         hot = jnp.concatenate(
             [
@@ -406,6 +389,55 @@
         )
         lat_of.append(lat_weight(at_row - lanes, loc_lat))
 
+    describe(0)
+
+    def advect(k):
+        no_north, no_south = la == lats - 1, la == 0
+        for r in range(rows):
+            here = cells_in[k * rows + r]
+            if r + 1 < rows:
+                north = cells_in[k * rows + r + 1]
+            else:
+                north = jnp.where(no_north, 0.0, from_north[k])
+            if r > 0:
+                south = cells_in[k * rows + r - 1]
+            else:
+                south = jnp.where(no_south, 0.0, from_south[k])
+            adv_out[k * rows + r] = advect_row(
+                here, north, south, edge_in[0, k, :, r : r + 1], edge_in[1, k, :, r : r + 1],
+                east_courant[r : r + 1, :], north_courant[r : r + 1, :],
+            )
+
+    for copy in halos[0]:
+        copy.wait_recv()
+    advect(0)
+    spot = iota((tile_room, cols), 1).astype(jnp.float32)
+    picked = jnp.zeros((tile_room, members), jnp.float32)
+    for r in range(rows):
+        chosen = one_hot((slot_col == spot) & (slot_row == r))
+        picked = picked + dot_t(chosen, adv_out[r], highest)
+    picked = jnp.concatenate(
+        [picked, jnp.zeros((tile_room, cols - members), jnp.float32)], axis=1
+    )
+    lat_own[...] = packed(picked)
+    lat_copies = []
+    for d in lat_steps:
+        copy = pltpu.make_async_remote_copy(
+            src_ref=lat_own, dst_ref=lat_in.at[d - 1], send_sem=lat_send.at[d - 1],
+            recv_sem=lat_recv.at[d - 1], device_id=at(d, 0), device_id_type=mesh_ids,
+        )
+        copy.start()
+        lat_copies.append(copy)
+
+    for k in range(1, channels):
+        for load in loads[k]:
+            load.wait()
+        pack_edges(k)
+        for copy in halos[k]:
+            copy.start()
+    for b in range(1, batches):
+        describe(b)
+
     def lon_field(b, k):
         return jnp.concatenate(
             [
@@ -420,21 +452,27 @@
 
     for copy in lat_copies:
         copy.wait_recv()
-    parts = jnp.concatenate([lat_own[...]] + [lat_in[d] for d in range(lats - 1)], axis=0)
+    parts = [unpacked(lat_own[...])] + [unpacked(lat_in[d]) for d in range(lats - 1)]
+    parts = jnp.concatenate(parts, axis=0)
     column = jnp.dot(move, parts, precision=highest, preferred_element_type=jnp.float32)
-    col_own[...] = column
+    for b in range(batches):
+        lon_in[reach, packed_room * b : packed_room * (b + 1)] = packed(
+            column[room * b : room * (b + 1)]
+        )
     lon_copies = []
     for i, d in enumerate(lon_steps):
-        size = room * (reach + 1 - abs(d))
-        size = min(size, room * batches)
+        part = pl.ds(0, prior_rows(d))
         copy = pltpu.make_async_remote_copy(
-            src_ref=col_own.at[pl.ds(0, size)], dst_ref=lon_in.at[reach - d, pl.ds(0, size)],
+            src_ref=lon_in.at[reach, part], dst_ref=lon_in.at[reach - d, part],
             send_sem=lon_send.at[i], recv_sem=lon_recv.at[i],
             device_id=at(0, d), device_id_type=mesh_ids,
         )
         copy.start()
         lon_copies.append(copy)
-    prior_out[reach] = column
+    for k in range(1, channels):
+        for copy in halos[k]:
+            copy.wait_recv()
+        advect(k)
 
     for (b, k), i in pair_ids.items():
         later = later_batches(b, k)
@@ -460,13 +498,9 @@
         too_many = jnp.maximum(too_many, jnp.sum(tally, axis=0, keepdims=True) - room)
     too_many = jnp.maximum(too_many, jnp.max(in_tile, axis=0, keepdims=True) - tile_room)
     overflow[0, 0] = jnp.max(too_many).astype(jnp.int32)
-    for i, d in enumerate(lon_steps):
-        lon_copies[i].wait_recv()
-    for d in lon_steps:
-        size = min(room * (reach + 1 - abs(d)), room * batches)
-        prior_out[reach - d, :size] = lon_in[reach - d, :size]
-        if size < room * batches:
-            prior_out[reach - d, size:] = jnp.zeros((room * batches - size, cols), jnp.float32)
+    for copy in lon_copies:
+        copy.wait_recv()
+    prior_out[...] = lon_in[...]
     for copies in (*halos, lat_copies, lon_copies):
         for copy in copies:
             copy.wait_send()
@@ -478,7 +512,7 @@
     vmem = pl.BlockSpec(memory_space=pltpu.VMEM)
     smem = pl.BlockSpec(memory_space=pltpu.SMEM)
     f32 = jnp.float32
-    slots = room * batches
+    slots = packed_room * batches
     return pl.pallas_call(
         exchange_kernel,
         name="exchange",
@@ -505,9 +539,8 @@
             pltpu.VMEM((channels, members, cols), f32),
             pltpu.VMEM((2, channels, members, cols), f32),
             pltpu.VMEM((2, channels, members, cols), f32),
-            pltpu.VMEM((tile_room, cols), f32),
-            pltpu.VMEM((lats - 1, tile_room, cols), f32),
-            pltpu.VMEM((slots, cols), f32),
+            pltpu.VMEM((packed_room, cols), f32),
+            pltpu.VMEM((lats - 1, packed_room, cols), f32),
             pltpu.VMEM((2 * reach + 1, slots, cols), f32),
             pltpu.SemaphoreType.DMA((channels * rows,)),
             pltpu.SemaphoreType.DMA((4 * channels,)),
@@ -527,7 +560,11 @@
 
 
 def update_kernel(adv, priors, obs_terms, pair_weights, cell_weights, out, field, slots, sem):
-    slots[...] = priors[...]
+    for k in range(-reach, reach + 1):
+        for b in range(batches):
+            if abs(k) <= spans[b]:
+                part = priors[reach + k, packed_room * b : packed_room * (b + 1)]
+                slots[reach + k, room * b : room * (b + 1)] = unpacked(part)
     lane = iota((1, cols), 1)
     is_member = lane < members
     unused = jnp.zeros((cols - 3 * room, cols), jnp.float32)
@@ -630,7 +667,7 @@
             pltpu.VMEM((2 * reach + 1, room * batches, cols), jnp.float32),
             pltpu.SemaphoreType.DMA((channels * rows,)),
         ],
-        compiler_params=pltpu.CompilerParams(vmem_limit_bytes=32 << 20),
+        compiler_params=pltpu.CompilerParams(vmem_limit_bytes=61 << 20),
     )(*operands)
 
 

time: 40.6 us -> 38.3 us (0.943)
  Pallas kernels: 38.6 us -> 37 us
  local copies, waits for them, and re-layouts: 0.94 us -> 0 us
    pallas_call x1, Pallas kernels: 29.6 us -> 27.8 us  [exchange(): pl.pallas_call(exchange_kernel, name='exchange', out_shape=(jax.ShapeDtyp...]
    unnamed x2 -> x0, local copies, waits for them, and re-layouts: 0.94 us -> none
where the time goes in v4:
time: 38.3 us; the launch traced here: 38.1 us
  Pallas kernels  37 us (97%)
  between operations  0.87 us (2%)
    pallas_call x1, Pallas kernels, exchange(): pl.pallas_call(exchange_kernel, name='exchange', out_shape=(jax.ShapeDtyp...  27.8 us
    pallas_call x1, Pallas kernels, update(): pl.pallas_call(update_kernel, name='update', out_shape=jax.ShapeDtypeStru...  9.23 us

profile of v4, /device:TPU:1, one launch (start us, length us, event | category | flops | bytes accessed | tf_op | source)
XLA Modules:
  0.0 38.1 jit_solution(11275089792290375533)
XLA Ops:
  0.0 27.8 %exchange.1 = (f32[24,80,128]{2,1,0:T(8,128)S(1)}, f32[9,64,128]{2,1,0:T(8,128)S(1)}, f32[576,8]{1,0:T(8,128)}, f32[15,72,128]{2,1,0:T(8,128)S(1)}, f32[4,8,72,128]{3,2,1,0:T(8,128)S(1)}, /*index=5*/s32[1,1]{1,0:T(1,128)}) custom-call(f32[80,3,8,128]{3,2,1,0:T(8,128)} %state.1, f32[8,128]{1,0:T(8,128)} %east_courant_in.1, f32[8,128]{1,0:T(8,128)} %north_courant_in.1, ...), custom_call_target="tpu_custom_call" | custom-call | tf_op jit(solution)/shard_map/exchange/pallas_call | solution.py:516
  28.5 9.5 %conditional.1 = (f32[80,3,8,128]{3,2,1,0:T(8,128)}) conditional(s32[]{:T(128)} %bitcast.1, (f32[24,80,128]{2,1,0:T(8,128)S(1)}, f32[9,64,128]{2,1,0:T(8,128)S(1)}, f32[576,8]{1,0:T(8,128)}, f32[15,72,128]{2,1,0:T(8,128)S(1)}, f32[4,8,72,128]{3,2,1,0:T(8,128)S(1)}) %tuple.33, (f32[8,128]{1,0:T(8,128)}, f32[80,3,8,128]{3,2,1,0:T(8,128)}, ...), branch_computations={%region_0.0_spmd, %region_1.9_spmd} | conditional | flops 1783096704 | bytes 50050640 | solution.py:676
  28.5 9.2 %update.1 = f32[80,3,8,128]{3,2,1,0:T(8,128)} custom-call(f32[24,80,128]{2,1,0:T(8,128)S(1)} %get-tuple-element.293.adv, f32[9,64,128]{2,1,0:T(8,128)S(1)} %get-tuple-element.294.priors, f32[576,8]{1,0:T(8,128)} %get-tuple-element.295.obs_terms, f32[15,72,128]{2,1,0:T(8,128)S(1)} %get-tuple-element.296.pair_weights, ...), custom_call_target="tpu_custom_call" | custom-call | tf_op jit(solution)/shard_map/cond/branch_0_fun/update/pallas_call | solution.py:659

commit v5 on v4

--- a/solution.py
+++ b/solution.py
@@ -408,14 +408,36 @@
                 east_courant[r : r + 1, :], north_courant[r : r + 1, :],
             )
 
+    spot = iota((tile_room, cols), 1).astype(jnp.float32)
+    in_col = slot_col == spot
+    nothing = jnp.zeros((members, cols), jnp.float32)
+    picked = jnp.zeros((tile_room, members), jnp.float32)
+    winds = jnp.zeros((tile_room, cols), jnp.float32)
+    for r in range(rows):
+        chosen = one_hot(in_col & (slot_row == r))
+        winds = winds + chosen * east_courant[r : r + 1, :]
+        inside = advect_row(
+            cells_in[r], cells_in[r + 1] if r + 1 < rows else nothing,
+            cells_in[r - 1] if r > 0 else nothing, 0.0, 0.0,
+            east_courant[r : r + 1, :], north_courant[r : r + 1, :],
+        )
+        picked = picked + dot_t(chosen, inside, highest)
+    wind = jnp.sum(winds, axis=1, keepdims=True)
+    last_row = one_hot(in_col & (slot_row == rows - 1) & (la < lats - 1))
+    first_row = one_hot(in_col & (slot_row == 0) & (la > 0))
+    to_north = last_row * (diffusion_number - 0.5 * north_courant[rows - 1 : rows, :])
+    to_south = first_row * (diffusion_number + 0.5 * north_courant[0:1, :])
+    to_east = one_hot((slot_row == spot) & (slot_col == cols - 1))
+    to_east = to_east * (diffusion_number - 0.5 * wind)
+    to_west = one_hot((slot_row == spot) & (slot_col == 0)) * (diffusion_number + 0.5 * wind)
     for copy in halos[0]:
         copy.wait_recv()
-    advect(0)
-    spot = iota((tile_room, cols), 1).astype(jnp.float32)
-    picked = jnp.zeros((tile_room, members), jnp.float32)
-    for r in range(rows):
-        chosen = one_hot((slot_col == spot) & (slot_row == r))
-        picked = picked + dot_t(chosen, adv_out[r], highest)
+    beyond = [
+        (to_north, from_north[0]), (to_south, from_south[0]),
+        (to_east, edge_in[1, 0]), (to_west, edge_in[0, 0]),
+    ]
+    for shares, values in beyond:
+        picked = picked + dot_t(shares, values, highest)
     picked = jnp.concatenate(
         [picked, jnp.zeros((tile_room, cols - members), jnp.float32)], axis=1
     )
@@ -429,6 +451,7 @@
         copy.start()
         lat_copies.append(copy)
 
+    advect(0)
     for k in range(1, channels):
         for load in loads[k]:
             load.wait()
@@ -569,7 +592,7 @@
     is_member = lane < members
     unused = jnp.zeros((cols - 3 * room, cols), jnp.float32)
     unused_three = jnp.zeros((cols - 3 * room, 3 * cols), jnp.float32)
-    chunk = 4
+    chunk = 24
     copies = []
     for b in range(batches):
         mine = slice(b * room, (b + 1) * room)

time: 38.3 us -> 34.9 us (0.911)
  Pallas kernels: 37 us -> 33.6 us
    pallas_call x1, Pallas kernels: 9.23 us -> 6.37 us  [update(): pl.pallas_call(update_kernel, name='update', out_shape=jax.ShapeDtypeStru...]
    pallas_call x1, Pallas kernels: 27.8 us -> 27.2 us  [exchange(): pl.pallas_call(exchange_kernel, name='exchange', out_shape=(jax.ShapeDtyp...]
where the time goes in v5:
time: 34.9 us; the launch traced here: 34.7 us
  Pallas kernels  33.6 us (96%)
  between operations  0.87 us (2%)
    pallas_call x1, Pallas kernels, exchange(): pl.pallas_call(exchange_kernel, name='exchange', out_shape=(jax.ShapeDtyp...  27.2 us
    pallas_call x1, Pallas kernels, update(): pl.pallas_call(update_kernel, name='update', out_shape=jax.ShapeDtypeStru...  6.37 us

profile of v5, /device:TPU:1, one launch (start us, length us, event | category | flops | bytes accessed | tf_op | source)
XLA Modules:
  0.0 34.7 jit_solution(13174434314978144661)
XLA Ops:
  0.0 27.2 %exchange.1 = (f32[24,80,128]{2,1,0:T(8,128)S(1)}, f32[9,64,128]{2,1,0:T(8,128)S(1)}, f32[576,8]{1,0:T(8,128)}, f32[15,72,128]{2,1,0:T(8,128)S(1)}, f32[4,8,72,128]{3,2,1,0:T(8,128)S(1)}, /*index=5*/s32[1,1]{1,0:T(1,128)}) custom-call(f32[80,3,8,128]{3,2,1,0:T(8,128)} %state.1, f32[8,128]{1,0:T(8,128)} %east_courant_in.1, f32[8,128]{1,0:T(8,128)} %north_courant_in.1, ...), custom_call_target="tpu_custom_call" | custom-call | tf_op jit(solution)/shard_map/exchange/pallas_call | solution.py:539
  27.9 6.6 %conditional.1 = (f32[80,3,8,128]{3,2,1,0:T(8,128)}) conditional(s32[]{:T(128)} %bitcast.1, (f32[24,80,128]{2,1,0:T(8,128)S(1)}, f32[9,64,128]{2,1,0:T(8,128)S(1)}, f32[576,8]{1,0:T(8,128)}, f32[15,72,128]{2,1,0:T(8,128)S(1)}, f32[4,8,72,128]{3,2,1,0:T(8,128)S(1)}) %tuple.33, (f32[8,128]{1,0:T(8,128)}, f32[80,3,8,128]{3,2,1,0:T(8,128)}, ...), branch_computations={%region_0.0_spmd, %region_1.9_spmd} | conditional | flops 1783096704 | bytes 50050640 | solution.py:699
  27.9 6.4 %update.1 = f32[80,3,8,128]{3,2,1,0:T(8,128)} custom-call(f32[24,80,128]{2,1,0:T(8,128)S(1)} %get-tuple-element.293.adv, f32[9,64,128]{2,1,0:T(8,128)S(1)} %get-tuple-element.294.priors, f32[576,8]{1,0:T(8,128)} %get-tuple-element.295.obs_terms, f32[15,72,128]{2,1,0:T(8,128)S(1)} %get-tuple-element.296.pair_weights, ...), custom_call_target="tpu_custom_call" | custom-call | tf_op jit(solution)/shard_map/cond/branch_0_fun/update/pallas_call | solution.py:682
